TPU v7x, 32 devices: a whole 2x2x4 slice. The times are simulated.
32 devices in a mesh: fsdp: 8 (over z, y), dp: 4 (over x, core).
Axes of the slice: x: 2, y: 2, z: 4, core: 2. Of those that a mesh axis runs over, the one named last changes fastest.
Arguments:
- tokens: bfloat16 [32, 1024, 768], P(('fsdp', 'dp')), may hold values from -6 to 6
- segment_ids: int32 [32, 1024], P(('fsdp', 'dp')), may hold values from 0 to 20, never falling along the last dimension, each value on 1 to 49 neighbouring positions
- cotangent: bfloat16 [32, 1024, 768], P(('fsdp', 'dp')), may hold values from -6 to 6
- ln1_gain: bfloat16 [768], P('fsdp'), may hold values from 0.25 to 1.75
- ln1_bias: bfloat16 [768], P('fsdp'), may hold values from -1.75 to 1.75
- qkv_weight: bfloat16 [768, 2304], P('fsdp'), may hold values from -0.21875 to 0.21875
- query_bias: bfloat16 [768], P('fsdp'), may hold values from -1.75 to 1.75
- value_bias: bfloat16 [768], P('fsdp'), may hold values from -1.75 to 1.75
- proj_weight: bfloat16 [768, 768], P('fsdp'), may hold values from -0.875 to 0.875
- proj_bias: bfloat16 [768], P('fsdp'), may hold values from -1.75 to 1.75
- ln2_gain: bfloat16 [768], P('fsdp'), may hold values from 0.25 to 1.75
- ln2_bias: bfloat16 [768], P('fsdp'), may hold values from -1.75 to 1.75
- fc1_weight: bfloat16 [768, 3072], P('fsdp'), may hold values from -0.21875 to 0.21875
- fc1_bias: bfloat16 [3072], P('fsdp'), may hold values from -1.75 to 1.75
- fc2_weight: bfloat16 [3072, 768], P('fsdp'), may hold values from -0.15625 to 0.15625
- fc2_bias: bfloat16 [768], P('fsdp'), may hold values from -1.75 to 1.75
Outputs:
- layer_out: bfloat16 [32, 1024, 768], P(('fsdp', 'dp'))
- input_grad: float32 [32, 1024, 768], P(('fsdp', 'dp'))
- grad_ln1_gain: float32 [768], P('fsdp')
- grad_ln1_bias: float32 [768], P('fsdp')
- grad_qkv_weight: float32 [768, 2304], P('fsdp')
- grad_query_bias: float32 [768], P('fsdp')
- grad_value_bias: float32 [768], P('fsdp')
- grad_proj_weight: float32 [768, 768], P('fsdp')
- grad_proj_bias: float32 [768], P('fsdp')
- grad_ln2_gain: float32 [768], P('fsdp')
- grad_ln2_bias: float32 [768], P('fsdp')
- grad_fc1_weight: float32 [768, 3072], P('fsdp')
- grad_fc1_bias: float32 [3072], P('fsdp')
- grad_fc2_weight: float32 [3072, 768], P('fsdp')
- grad_fc2_bias: float32 [768], P('fsdp')
Inputs may be any that keep to these rules, and one draw needn't show every extreme that they name: `segment_ids`: within a row the ids never fall and each id covers 1 to 49 consecutive positions.
All inputs are finite; a program needn't handle non-finite values.
Results may differ from a plain program's by a relative error of at most 0.015.
Values may be sent and summed in bfloat16 or wider, within the bound.
No kernel may reach another device: no remote copies, remote signals or barrier semaphores. Data moves between devices by JAX's collectives and lax.ppermute only.
A program may use at most 256 MiB of HBM per device.

v0:
```python
import jax
import jax.numpy as jnp
from jax import lax
from jax.sharding import PartitionSpec as P

HEADS = 12
HD = 64


epsilon = 1e-06
masked_fill = -1e30


def layer_norm(values, gain, shift):
    row_mean = jnp.mean(values, axis=-1, keepdims=True)
    centred = values - row_mean
    variance = jnp.mean(centred * centred, axis=-1, keepdims=True)
    return centred * lax.rsqrt(variance + epsilon) * gain + shift


def exact_gelu(values):
    return jax.nn.gelu(values, approximate=False)


def masked_scores(query_part, key_row, seg_part, seg_row, scale):
    raw = (
        jnp.einsum("qhd,khd->hqk", query_part, key_row, preferred_element_type=jnp.float32) * scale
    )
    same = seg_part[:, None] == seg_row[None, :]
    return jnp.where(same[None], raw, masked_fill)


def column_sum(values):
    return jnp.sum(values.astype(jnp.float32), axis=0)


def per_device(
    tokens,
    segment_ids,
    cotangent,
    ln1_gain,
    ln1_bias,
    qkv_weight,
    query_bias,
    value_bias,
    proj_weight,
    proj_bias,
    ln2_gain,
    ln2_bias,
    fc1_weight,
    fc1_bias,
    fc2_weight,
    fc2_bias,
):
    rows_here, seq_len, width = tokens.shape
    block = min(512, seq_len)
    blocks = seq_len // block
    scale = HD ** (-0.5)
    (
        whole_ln1_gain,
        whole_ln1_bias,
        whole_qkv,
        whole_query_bias,
        whole_value_bias,
        whole_proj,
        whole_proj_bias,
        whole_ln2_gain,
        whole_ln2_bias,
        whole_fc1,
        whole_fc1_bias,
        whole_fc2,
        whole_fc2_bias,
    ) = (
        lax.all_gather(ln1_gain, "fsdp", axis=0, tiled=True),
        lax.all_gather(ln1_bias, "fsdp", axis=0, tiled=True),
        lax.all_gather(qkv_weight, "fsdp", axis=0, tiled=True),
        lax.all_gather(query_bias, "fsdp", axis=0, tiled=True),
        lax.all_gather(value_bias, "fsdp", axis=0, tiled=True),
        lax.all_gather(proj_weight, "fsdp", axis=0, tiled=True),
        lax.all_gather(proj_bias, "fsdp", axis=0, tiled=True),
        lax.all_gather(ln2_gain, "fsdp", axis=0, tiled=True),
        lax.all_gather(ln2_bias, "fsdp", axis=0, tiled=True),
        lax.all_gather(fc1_weight, "fsdp", axis=0, tiled=True),
        lax.all_gather(fc1_bias, "fsdp", axis=0, tiled=True),
        lax.all_gather(fc2_weight, "fsdp", axis=0, tiled=True),
        lax.all_gather(fc2_bias, "fsdp", axis=0, tiled=True),
    )
    flat = tokens.reshape(-1, width).astype(jnp.float32)
    normed_one, norm_one_back = jax.vjp(
        layer_norm, flat, whole_ln1_gain.astype(jnp.float32), whole_ln1_bias.astype(jnp.float32)
    )
    normed_one = normed_one.astype(jnp.bfloat16)
    qkv_shift = jnp.concatenate(
        [
            whole_query_bias.astype(jnp.float32),
            jnp.zeros((width,), jnp.float32),
            whole_value_bias.astype(jnp.float32),
        ]
    )
    qkv_rounded = (
        jnp.dot(normed_one, whole_qkv, preferred_element_type=jnp.float32) + qkv_shift
    ).astype(jnp.bfloat16)
    qkv_heads = qkv_rounded.reshape(rows_here, seq_len, 3, HEADS, HD)
    query_all = qkv_heads[:, :, 0]
    key_all = qkv_heads[:, :, 1]
    value_all = qkv_heads[:, :, 2]

    def attend_row(items):
        query_row, key_row, value_row, seg_row = items
        query_blocks = query_row.reshape(blocks, block, HEADS, HD)
        seg_blocks = seg_row.reshape(blocks, block)

        def attend_block(pieces):
            query_part, seg_part = pieces
            masked = masked_scores(query_part, key_row, seg_part, seg_row, scale)
            row_max = jnp.max(masked, axis=-1, keepdims=True)
            expo = jnp.exp(masked - row_max)
            total = jnp.sum(expo, axis=-1, keepdims=True)
            probs_low = (expo / total).astype(jnp.bfloat16)
            context_part = jnp.einsum(
                "hqk,khd->qhd", probs_low, value_row, preferred_element_type=jnp.float32
            )
            return (context_part, row_max + jnp.log(total))

        context_row, lse_row = lax.map(attend_block, (query_blocks, seg_blocks))
        return (context_row.reshape(seq_len, width), lse_row)

    context, lse_all = lax.map(attend_row, (query_all, key_all, value_all, segment_ids))
    context_rounded = context.reshape(-1, width).astype(jnp.bfloat16)
    attended = jnp.dot(
        context_rounded, whole_proj, preferred_element_type=jnp.float32
    ) + whole_proj_bias.astype(jnp.float32)
    middle = flat + attended
    normed_two, norm_two_back = jax.vjp(
        layer_norm, middle, whole_ln2_gain.astype(jnp.float32), whole_ln2_bias.astype(jnp.float32)
    )
    normed_two = normed_two.astype(jnp.bfloat16)
    hidden = jnp.dot(
        normed_two, whole_fc1, preferred_element_type=jnp.float32
    ) + whole_fc1_bias.astype(jnp.float32)
    activated, gelu_back = jax.vjp(exact_gelu, hidden)
    activated = activated.astype(jnp.bfloat16)
    branch = jnp.dot(
        activated, whole_fc2, preferred_element_type=jnp.float32
    ) + whole_fc2_bias.astype(jnp.float32)
    layer_out = (middle + branch).astype(jnp.bfloat16).reshape(tokens.shape)
    back_qkv, back_proj, back_fc1, back_fc2 = (
        lax.all_gather(qkv_weight, "fsdp", axis=0, tiled=True),
        lax.all_gather(proj_weight, "fsdp", axis=0, tiled=True),
        lax.all_gather(fc1_weight, "fsdp", axis=0, tiled=True),
        lax.all_gather(fc2_weight, "fsdp", axis=0, tiled=True),
    )
    upstream = cotangent.reshape(-1, width).astype(jnp.float32)
    d_branch = upstream.astype(jnp.bfloat16)
    grad_fc2_bias = column_sum(d_branch)
    grad_fc2_weight = jnp.einsum(
        "tf,td->fd", activated, d_branch, preferred_element_type=jnp.float32
    )
    d_activated = jnp.einsum("td,fd->tf", d_branch, back_fc2, preferred_element_type=jnp.float32)
    d_hidden = gelu_back(d_activated)[0].astype(jnp.bfloat16)
    grad_fc1_bias = column_sum(d_hidden)
    grad_fc1_weight = jnp.einsum(
        "td,tf->df", normed_two, d_hidden, preferred_element_type=jnp.float32
    )
    d_norm_two = jnp.einsum("tf,df->td", d_hidden, back_fc1, preferred_element_type=jnp.float32)
    d_mid_term, grad_ln2_gain, grad_ln2_bias = norm_two_back(d_norm_two)
    d_middle = upstream + d_mid_term
    d_attended = d_middle.astype(jnp.bfloat16)
    grad_proj_bias = column_sum(d_attended)
    grad_proj_weight = jnp.einsum(
        "td,te->de", context_rounded, d_attended, preferred_element_type=jnp.float32
    )
    d_context = jnp.einsum(
        "te,de->td", d_attended, back_proj, preferred_element_type=jnp.float32
    ).astype(jnp.bfloat16)
    d_context_rows = d_context.reshape(rows_here, seq_len, HEADS, HD)

    def attend_back_row(items):
        query_row, key_row, value_row, seg_row, lse_row, dctx_row = items
        query_blocks = query_row.reshape(blocks, block, HEADS, HD)
        seg_blocks = seg_row.reshape(blocks, block)
        dctx_blocks = dctx_row.reshape(blocks, block, HEADS, HD)

        def back_block(carry, pieces):
            key_grad, value_grad = carry
            query_part, seg_part, lse_part, dctx_part = pieces
            masked = masked_scores(query_part, key_row, seg_part, seg_row, scale)
            probs = jnp.exp(masked - lse_part)
            value_grad = value_grad + jnp.einsum(
                "hqk,qhd->khd",
                probs.astype(jnp.bfloat16),
                dctx_part,
                preferred_element_type=jnp.float32,
            )
            prob_grad = jnp.einsum(
                "qhd,khd->hqk", dctx_part, value_row, preferred_element_type=jnp.float32
            )
            score_grad = (
                probs * (prob_grad - jnp.sum(prob_grad * probs, axis=-1, keepdims=True))
            ).astype(jnp.bfloat16)
            query_grad = (
                jnp.einsum("hqk,khd->qhd", score_grad, key_row, preferred_element_type=jnp.float32)
                * scale
            )
            key_grad = (
                key_grad
                + jnp.einsum(
                    "hqk,qhd->khd", score_grad, query_part, preferred_element_type=jnp.float32
                )
                * scale
            )
            return ((key_grad, value_grad), query_grad)

        zero_grad = jnp.zeros((seq_len, HEADS, HD), jnp.float32)
        (key_grad, value_grad), query_grad = lax.scan(
            back_block, (zero_grad, zero_grad), (query_blocks, seg_blocks, lse_row, dctx_blocks)
        )
        return jnp.concatenate(
            [
                query_grad.reshape(seq_len, width),
                key_grad.reshape(seq_len, width),
                value_grad.reshape(seq_len, width),
            ],
            axis=1,
        )

    d_qkv = lax.map(
        attend_back_row, (query_all, key_all, value_all, segment_ids, lse_all, d_context_rows)
    )
    d_qkv = d_qkv.reshape(-1, 3 * width).astype(jnp.bfloat16)
    grad_query_bias = column_sum(d_qkv[:, :width])
    grad_value_bias = column_sum(d_qkv[:, 2 * width :])
    grad_qkv_weight = jnp.einsum("td,te->de", normed_one, d_qkv, preferred_element_type=jnp.float32)
    d_norm_one = jnp.einsum("te,de->td", d_qkv, back_qkv, preferred_element_type=jnp.float32)
    d_token_term, grad_ln1_gain, grad_ln1_bias = norm_one_back(d_norm_one)
    input_grad = (d_middle + d_token_term).reshape(tokens.shape)
    pieces_all = (
        lax.psum_scatter(grad_ln1_gain, ("fsdp", "dp"), scatter_dimension=0, tiled=True),
        lax.psum_scatter(grad_ln1_bias, ("fsdp", "dp"), scatter_dimension=0, tiled=True),
        lax.psum_scatter(grad_qkv_weight, ("fsdp", "dp"), scatter_dimension=0, tiled=True),
        lax.psum_scatter(grad_query_bias, ("fsdp", "dp"), scatter_dimension=0, tiled=True),
        lax.psum_scatter(grad_value_bias, ("fsdp", "dp"), scatter_dimension=0, tiled=True),
        lax.psum_scatter(grad_proj_weight, ("fsdp", "dp"), scatter_dimension=0, tiled=True),
        lax.psum_scatter(grad_proj_bias, ("fsdp", "dp"), scatter_dimension=0, tiled=True),
        lax.psum_scatter(grad_ln2_gain, ("fsdp", "dp"), scatter_dimension=0, tiled=True),
        lax.psum_scatter(grad_ln2_bias, ("fsdp", "dp"), scatter_dimension=0, tiled=True),
        lax.psum_scatter(grad_fc1_weight, ("fsdp", "dp"), scatter_dimension=0, tiled=True),
        lax.psum_scatter(grad_fc1_bias, ("fsdp", "dp"), scatter_dimension=0, tiled=True),
        lax.psum_scatter(grad_fc2_weight, ("fsdp", "dp"), scatter_dimension=0, tiled=True),
        lax.psum_scatter(grad_fc2_bias, ("fsdp", "dp"), scatter_dimension=0, tiled=True),
    )
    (
        piece_ln1_gain,
        piece_ln1_bias,
        piece_qkv,
        piece_query_bias,
        piece_value_bias,
        piece_proj,
        piece_proj_bias,
        piece_ln2_gain,
        piece_ln2_bias,
        piece_fc1,
        piece_fc1_bias,
        piece_fc2,
        piece_fc2_bias,
    ) = pieces_all
    summed = (
        lax.all_gather(piece_ln1_gain.astype(jnp.bfloat16), "dp", axis=0, tiled=True).astype(
            piece_ln1_gain.dtype
        ),
        lax.all_gather(piece_ln1_bias.astype(jnp.bfloat16), "dp", axis=0, tiled=True).astype(
            piece_ln1_bias.dtype
        ),
        lax.all_gather(piece_qkv.astype(jnp.bfloat16), "dp", axis=0, tiled=True).astype(
            piece_qkv.dtype
        ),
        lax.all_gather(piece_query_bias.astype(jnp.bfloat16), "dp", axis=0, tiled=True).astype(
            piece_query_bias.dtype
        ),
        lax.all_gather(piece_value_bias.astype(jnp.bfloat16), "dp", axis=0, tiled=True).astype(
            piece_value_bias.dtype
        ),
        lax.all_gather(piece_proj.astype(jnp.bfloat16), "dp", axis=0, tiled=True).astype(
            piece_proj.dtype
        ),
        lax.all_gather(piece_proj_bias.astype(jnp.bfloat16), "dp", axis=0, tiled=True).astype(
            piece_proj_bias.dtype
        ),
        lax.all_gather(piece_ln2_gain.astype(jnp.bfloat16), "dp", axis=0, tiled=True).astype(
            piece_ln2_gain.dtype
        ),
        lax.all_gather(piece_ln2_bias.astype(jnp.bfloat16), "dp", axis=0, tiled=True).astype(
            piece_ln2_bias.dtype
        ),
        lax.all_gather(piece_fc1.astype(jnp.bfloat16), "dp", axis=0, tiled=True).astype(
            piece_fc1.dtype
        ),
        lax.all_gather(piece_fc1_bias.astype(jnp.bfloat16), "dp", axis=0, tiled=True).astype(
            piece_fc1_bias.dtype
        ),
        lax.all_gather(piece_fc2.astype(jnp.bfloat16), "dp", axis=0, tiled=True).astype(
            piece_fc2.dtype
        ),
        lax.all_gather(piece_fc2_bias.astype(jnp.bfloat16), "dp", axis=0, tiled=True).astype(
            piece_fc2_bias.dtype
        ),
    )
    return (
        layer_out,
        input_grad,
        summed[0],
        summed[1],
        summed[2],
        summed[3],
        summed[4],
        summed[5],
        summed[6],
        summed[7],
        summed[8],
        summed[9],
        summed[10],
        summed[11],
        summed[12],
    )


def solution(mesh):
    placed = (
        P(("fsdp", "dp"), None, None),
        P(("fsdp", "dp"), None),
        P(("fsdp", "dp"), None, None),
        P("fsdp"),
        P("fsdp"),
        P("fsdp", None),
        P("fsdp"),
        P("fsdp"),
        P("fsdp", None),
        P("fsdp"),
        P("fsdp"),
        P("fsdp"),
        P("fsdp", None),
        P("fsdp"),
        P("fsdp", None),
        P("fsdp"),
    )
    return jax.shard_map(
        per_device,
        mesh=mesh,
        in_specs=placed,
        out_specs=(
            P(("fsdp", "dp"), None, None),
            P(("fsdp", "dp"), None, None),
            P("fsdp"),
            P("fsdp"),
            P("fsdp", None),
            P("fsdp"),
            P("fsdp"),
            P("fsdp", None),
            P("fsdp"),
            P("fsdp"),
            P("fsdp"),
            P("fsdp", None),
            P("fsdp"),
            P("fsdp", None),
            P("fsdp"),
        ),
        check_vma=False,
    )
```

profile of v0, /device:TPU:0, one launch (start us, length us, event | category | flops | bytes accessed | tf_op | source)
XLA Modules:
  0.0 932.9 jit_solution(7279127503173805314)
XLA Ops:
  19.3 40.0 %all-reduce.27 = (bf16[768]{0:T(1024)(128)(2,1)S(1)}, bf16[768]{0:T(1024)(128)(2,1)S(1)}, bf16[768]{0:T(1024)(128)(2,1)S(1)}, bf16[768]{0:T(1024)(128)(2,1)S(1)}...) all-reduce(bf16[768]{0:T(1024)(128)(2,1)S(1)} %dynamic-update-slice, ...), channel_id=1, replica_groups=mesh['fsdp'=8,'dp'=4] {'fsdp'}, use_global_device_ids=true, to_apply=%add.3 | all-reduce | flops 6144 | bytes 24576
  63.1 26.8 %all-gather = bf16[8,1,384]{2,1,0:T(2,128)(2,1)S(1)} all-gather(bf16[1,1,384]{2,1,0:T(2,128)(2,1)S(1)} %reshape.332), channel_id=1, replica_groups=mesh['fsdp'=8,'dp'=4] {'fsdp'}, dimensions={0}, use_global_device_ids=true | all-gather | bytes 6912 | tf_op jit(solution)/shard_map/all_gather | solution.py:84
  90.5 1.8 copy.59
  93.7 1.7 copy.64
  95.5 7.9 add_convert_fusion.1
  103.4 6.7 copy.60
  110.1 4.2 slice_bitcast_fusion
  114.3 2.3 reshape.273
  116.7 1.7 copy.61
  119.7 81.5 %while.45 = (s32[]{:T(128)}, bf16[2,512,12,64]{1,3,2,0:T(8,128)(2,1)}, f32[2,12,512,1]{2,1,3,0:T(8,128)S(1)}, s32[2,512]{1,0:T(2,128)S(1)}, s32[1024]{0:T(1024)S...) while((s32[]{:T(128)}, ...), condition=%wide.region_5.6_spmd, body=%wide.region_2.5_spmd.sunk | while | flops 1686628352 | bytes 190286000 | solution.py:125
  120.1 11.0 %fusion.125 = (f32[12,512]{1,0:T(8,128)S(1)}, f32[12,512,1024]{2,1,0:T(8,128)}) fusion(pred[512,1024]{1,0:T(8,128)(4,1)S(1)} %broadcast_compare_fusion.4, bf16[1024,12,64]{0,2,1:T(8,128)(2,1)S(1)} %get-tuple-element.540, bf16[2,512,12,64]{1,3,2,0:T(8,128)(2,1)S(1)} %get-tuple-element.539, s32[]{:T(128)S(6)} %copy.92), kind=kOutput, calls=%fused_computation.3.clone.1 | convolution fusion | flops 824174592 | bytes 28073988 | tf_op jit(solution)/shard_map/while/body/eval_jaxpr/while/body/eval_jaxpr/qhd,khd->hqk/dot_general | solution.py:27
  131.1 12.4 %fusion.126 = f32[12,512]{1,0:T(8,128)S(1)} fusion(f32[12,512,1024]{2,1,0:T(8,128)} %get-tuple-element.501, f32[12,512]{1,0:T(8,128)S(1)} %get-tuple-element.502, pred[512,1024]{1,0:T(8,128)(4,1)S(1)} %broadcast_compare_fusion.4), kind=kLoop, calls=%fused_computation.4.clone.1 | loop fusion | flops 25159680 | bytes 25739264 | tf_op jit(solution)/shard_map/while/body/eval_jaxpr/while/body/eval_jaxpr/reduce_sum | solution.py:118
  143.5 3.2 copy-done
  146.7 8.5 bitcast_dynamic-update-slice_fusion.6
  155.6 10.7 %fusion.125 = (f32[12,512]{1,0:T(8,128)S(1)}, f32[12,512,1024]{2,1,0:T(8,128)}) fusion(pred[512,1024]{1,0:T(8,128)(4,1)S(1)} %broadcast_compare_fusion.4, bf16[1024,12,64]{0,2,1:T(8,128)(2,1)S(1)} %get-tuple-element.540, bf16[2,512,12,64]{1,3,2,0:T(8,128)(2,1)S(1)} %get-tuple-element.539, s32[]{:T(128)S(6)} %copy.92), kind=kOutput, calls=%fused_computation.3.clone.1 | convolution fusion | flops 824174592 | bytes 28073988 | tf_op jit(solution)/shard_map/while/body/eval_jaxpr/while/body/eval_jaxpr/qhd,khd->hqk/dot_general | solution.py:27
  166.3 12.4 %fusion.126 = f32[12,512]{1,0:T(8,128)S(1)} fusion(f32[12,512,1024]{2,1,0:T(8,128)} %get-tuple-element.501, f32[12,512]{1,0:T(8,128)S(1)} %get-tuple-element.502, pred[512,1024]{1,0:T(8,128)(4,1)S(1)} %broadcast_compare_fusion.4), kind=kLoop, calls=%fused_computation.4.clone.1 | loop fusion | flops 25159680 | bytes 25739264 | tf_op jit(solution)/shard_map/while/body/eval_jaxpr/while/body/eval_jaxpr/reduce_sum | solution.py:118
  178.7 3.1 copy-done
  181.8 8.5 bitcast_dynamic-update-slice_fusion.6
  201.2 4.2 copy.62
  205.4 1.6 copy.76
  207.0 4.2 fusion.82
  212.0 37.9 %multiply_convert_fusion.1 = (bf16[1024,3072]{1,0:T(8,128)(2,1)}, f32[1024,3072]{1,0:T(8,128)}, f32[1024,3072]{1,0:T(8,128)}) fusion(f32[3072]{0:T(1024)S(1)} %bitcast.198, bf16[768,3072]{1,0:T(8,128)(2,1)} %all-gather.10.cloned.1.call-done, f32[1024,768]{0,1:T(8,128)S(1)} %get-tuple-element.383, f32[768]{0:T(1024)S(1)} %copy-done.47, ...), kind=kOutput, calls=%fused_computation.48 | convolution fusion | flops 5043388416 | bytes 39348224 | tf_op jit(solution)/shard_map/dot_general | solution.py:138
  249.9 30.4 %all-gather.12.cloned.1.call-done = bf16[3072,768]{1,0:T(8,128)(2,1)} async-done(((bf16[384,768]{1,0:T(8,128)(2,1)}), bf16[3072,768]{1,0:T(8,128)(2,1)}) %all-gather.12.cloned.1.call-update) | async-done | bytes 4718608 | tf_op jit(solution)/shard_map/all_gather | solution.py:85
  280.3 19.2 %convert_reduce_fusion = (f32[3072]{0:T(1024)}, bf16[1024,3072]{1,0:T(8,128)(2,1)}) fusion(f32[1024,3072]{1,0:T(8,128)} %get-tuple-element.372, bf16[3072,768]{1,0:T(8,128)(2,1)} %all-gather.12.cloned.1.call-done, bf16[1,1024,768]{2,1,0:T(8,128)(2,1)} %param.22, f32[1024,3072]{1,0:T(8,128)} %get-tuple-element.384, f32[3072]{0:T(1024)S(1)} %bitcast.199), kind=kOutput, calls=%fused_computation.46 | convolution fusion | flops 4885312512 | bytes 37773312 | tf_op jit(solution)/shard_map/td,fd->tf/dot_general | solution.py:159
  299.5 10.4 %fusion.84 = (f32[768]{0:T(1024)}, f32[1024,768]{1,0:T(8,128)}) fusion(bf16[1024,3072]{1,0:T(8,128)(2,1)} %get-tuple-element.390, bf16[768,3072]{1,0:T(8,128)(2,1)} %all-gather.10.cloned.1.call-done), kind=kOutput, calls=%fused_computation.144 | convolution fusion | flops 4832623616 | bytes 14158848 | tf_op jit(solution)/shard_map/tf,df->td/dot_general | solution.py:165
  309.8 3.5 copy.65
  313.4 3.5 multiply_reduce_fusion.1
  320.3 2.8 fusion.85
  323.1 2.7 convolution_convert_fusion
  327.9 1.5 copy.68
  330.7 169.1 %while.46 = (s32[]{:T(128)}, f32[1024,12,64]{0,2,1:T(8,128)}, f32[1024,12,64]{0,2,1:T(8,128)}, bf16[2,512,12,64]{1,3,2,0:T(8,128)(2,1)}, bf16[2,512,12,64]{1,3,2...) while((s32[]{:T(128)}, f32[1024,12,64]{0,2,1:T(8,128)}, ...), condition=%wide.region_12.13_spmd.clone, body=%wide.region_10.12_spmd.clone.sunk | while | flops 4125747200 | bytes 225634512 | solution.py:215
  331.3 11.6 %fusion.136 = f32[12,512,1024]{2,1,0:T(8,128)} fusion(bf16[1024,12,64]{0,2,1:T(8,128)(2,1)S(1)} %get-tuple-element.576, bf16[2,512,12,64]{1,3,2,0:T(8,128)(2,1)} %get-tuple-element.573, s32[]{:T(128)S(6)} %copy.102), kind=kOutput, calls=%fused_computation.30.clone.1 | convolution fusion | flops 805306368 | bytes 27525124 | tf_op jit(solution)/shard_map/while/body/eval_jaxpr/while/body/eval_jaxpr/qhd,khd->hqk/dot_general | solution.py:27
  343.0 13.8 %bitcast_add_fusion.5 = f32[1024,12,64]{0,2,1:T(8,128)} fusion(f32[1024,12,64]{0,2,1:T(8,128)} %get-tuple-element.558, f32[12,512,1024]{2,1,0:T(8,128)} %fusion.136, f32[12,512]{1,0:T(8,128)S(1)} %dynamic-slice_bitcast_fusion.2, pred[512,1024]{1,0:T(8,128)(4,1)S(1)} %broadcast_compare_fusion.5, pred[]{:T(512)S(6)} %compare.3, ...), kind=kOutput, calls=%fused_computation.22.clone.1 | convolution fusion | flops 832045056 | bytes 32800772 | tf_op jit(solution)/shard_map/while/body/eval_jaxpr/while/body/eval_jaxpr/hqk,qhd->khd/dot_general | solution.py:189
  356.7 18.3 %multiply_reduce_fusion.5 = (f32[12,512]{1,0:T(8,128)S(1)}, f32[12,512,1024]{2,1,0:T(8,128)}) fusion(f32[12,512,1024]{2,1,0:T(8,128)} %fusion.136, f32[12,512]{1,0:T(8,128)S(1)} %dynamic-slice_bitcast_fusion.2, pred[512,1024]{1,0:T(8,128)(4,1)S(1)} %broadcast_compare_fusion.5, bf16[1024,12,64]{0,2,1:T(8,128)(2,1)} %get-tuple-element.579, ...), kind=kOutput, calls=%fused_computation.17.clone.1 | convolution fusion | flops 836757504 | bytes 53264388 | tf_op jit(solution)/shard_map/while/body/eval_jaxpr/while/body/eval_jaxpr/qhd,khd->hqk/dot_general | solution.py:195
  375.0 22.0 %multiply_convert_fusion.3 = bf16[12,512,1024]{2,1,0:T(8,128)(2,1)} fusion(f32[12,512,1024]{2,1,0:T(8,128)} %get-tuple-element.514, f32[12,512,1024]{2,1,0:T(8,128)} %fusion.136, f32[12,512]{1,0:T(8,128)S(1)} %get-tuple-element.515, f32[12,512]{1,0:T(8,128)S(1)} %dynamic-slice_bitcast_fusion.2, pred[512,1024]{1,0:T(8,128)(4,1)S(1)} %broadcast_compare_fusion.5), kind=kLoop, calls=%fused_computation.16.clone.1 | loop fusion | flops 37748736 | bytes 63488000 | tf_op jit(solution)/shard_map/while/body/eval_jaxpr/while/body/eval_jaxpr/convert_element_type | solution.py:200
  397.0 9.5 %bitcast_dynamic-update-slice_fusion.8 = bf16[2,512,12,64]{1,3,2,0:T(8,128)(2,1)} fusion(bf16[2,512,12,64]{1,3,2,0:T(8,128)(2,1)} %get-tuple-element.559, s32[]{:T(128)S(6)} %copy.102, bf16[12,512,1024]{2,1,0:T(8,128)(2,1)} %multiply_convert_fusion.3, bf16[1024,12,64]{0,2,1:T(8,128)(2,1)S(1)} %get-tuple-element.576), kind=kOutput, calls=%fused_computation.24.clone.1 | convolution fusion | flops 805699584 | bytes 15728644 | tf_op jit(solution)/shard_map/while/body/eval_jaxpr/while/body/eval_jaxpr/hqk,khd->qhd/dot_general | solution.py:202
  406.5 8.6 bitcast_add_fusion.4
  415.5 11.5 %fusion.136 = f32[12,512,1024]{2,1,0:T(8,128)} fusion(bf16[1024,12,64]{0,2,1:T(8,128)(2,1)S(1)} %get-tuple-element.576, bf16[2,512,12,64]{1,3,2,0:T(8,128)(2,1)} %get-tuple-element.573, s32[]{:T(128)S(6)} %copy.102), kind=kOutput, calls=%fused_computation.30.clone.1 | convolution fusion | flops 805306368 | bytes 27525124 | tf_op jit(solution)/shard_map/while/body/eval_jaxpr/while/body/eval_jaxpr/qhd,khd->hqk/dot_general | solution.py:27
  427.0 14.3 %bitcast_add_fusion.5 = f32[1024,12,64]{0,2,1:T(8,128)} fusion(f32[1024,12,64]{0,2,1:T(8,128)} %get-tuple-element.558, f32[12,512,1024]{2,1,0:T(8,128)} %fusion.136, f32[12,512]{1,0:T(8,128)S(1)} %dynamic-slice_bitcast_fusion.2, pred[512,1024]{1,0:T(8,128)(4,1)S(1)} %broadcast_compare_fusion.5, pred[]{:T(512)S(6)} %compare.3, ...), kind=kOutput, calls=%fused_computation.22.clone.1 | convolution fusion | flops 832045056 | bytes 32800772 | tf_op jit(solution)/shard_map/while/body/eval_jaxpr/while/body/eval_jaxpr/hqk,qhd->khd/dot_general | solution.py:189
  441.3 18.1 %multiply_reduce_fusion.5 = (f32[12,512]{1,0:T(8,128)S(1)}, f32[12,512,1024]{2,1,0:T(8,128)}) fusion(f32[12,512,1024]{2,1,0:T(8,128)} %fusion.136, f32[12,512]{1,0:T(8,128)S(1)} %dynamic-slice_bitcast_fusion.2, pred[512,1024]{1,0:T(8,128)(4,1)S(1)} %broadcast_compare_fusion.5, bf16[1024,12,64]{0,2,1:T(8,128)(2,1)} %get-tuple-element.579, ...), kind=kOutput, calls=%fused_computation.17.clone.1 | convolution fusion | flops 836757504 | bytes 53264388 | tf_op jit(solution)/shard_map/while/body/eval_jaxpr/while/body/eval_jaxpr/qhd,khd->hqk/dot_general | solution.py:195
  459.4 21.2 %multiply_convert_fusion.3 = bf16[12,512,1024]{2,1,0:T(8,128)(2,1)} fusion(f32[12,512,1024]{2,1,0:T(8,128)} %get-tuple-element.514, f32[12,512,1024]{2,1,0:T(8,128)} %fusion.136, f32[12,512]{1,0:T(8,128)S(1)} %get-tuple-element.515, f32[12,512]{1,0:T(8,128)S(1)} %dynamic-slice_bitcast_fusion.2, pred[512,1024]{1,0:T(8,128)(4,1)S(1)} %broadcast_compare_fusion.5), kind=kLoop, calls=%fused_computation.16.clone.1 | loop fusion | flops 37748736 | bytes 63488000 | tf_op jit(solution)/shard_map/while/body/eval_jaxpr/while/body/eval_jaxpr/convert_element_type | solution.py:200
  480.7 9.5 %bitcast_dynamic-update-slice_fusion.8 = bf16[2,512,12,64]{1,3,2,0:T(8,128)(2,1)} fusion(bf16[2,512,12,64]{1,3,2,0:T(8,128)(2,1)} %get-tuple-element.559, s32[]{:T(128)S(6)} %copy.102, bf16[12,512,1024]{2,1,0:T(8,128)(2,1)} %multiply_convert_fusion.3, bf16[1024,12,64]{0,2,1:T(8,128)(2,1)S(1)} %get-tuple-element.576), kind=kOutput, calls=%fused_computation.24.clone.1 | convolution fusion | flops 805699584 | bytes 15728644 | tf_op jit(solution)/shard_map/while/body/eval_jaxpr/while/body/eval_jaxpr/hqk,khd->qhd/dot_general | solution.py:202
  490.2 9.5 %bitcast_add_fusion.4 = f32[1024,12,64]{0,2,1:T(8,128)} fusion(f32[1024,12,64]{0,2,1:T(8,128)} %get-tuple-element.557, bf16[12,512,1024]{2,1,0:T(8,128)(2,1)} %multiply_convert_fusion.3, pred[]{:T(512)S(6)} %compare.3, bf16[2,512,12,64]{1,3,2,0:T(8,128)(2,1)S(1)} %copy-done.5, s32[]{:T(128)S(6)} %copy.102), kind=kOutput, calls=%fused_computation.23.clone.1 | convolution fusion | flops 807665664 | bytes 19660804 | tf_op jit(solution)/shard_map/while/body/eval_jaxpr/while/body/eval_jaxpr/hqk,qhd->khd/dot_general | solution.py:207
  499.9 3.2 copy.69
  503.8 2.7 convert_reduce_fusion.4
  507.8 7.0 fusion.55
  515.5 10.6 %fusion.77 = f32[768,3072]{1,0:T(8,128)} fusion(bf16[1024,3072]{1,0:T(8,128)(2,1)} %get-tuple-element.390, f32[1024,768]{0,1:T(8,128)} %copy-done.10, f32[768]{0:T(1024)S(1)} %copy-done.48, f32[768]{0:T(1024)S(1)} %copy-done.40, f32[1024]{0:T(1024)S(1)} %copy-done.42, f32[1024]{0:T(1024)S(1)} %copy-done.32), kind=kOutput, calls=%fused_computation.139 | convolution fusion | flops 4835770368 | bytes 18888704 | tf_op jit(solution)/shard_map/td,tf->df/dot_general | solution.py:162
  526.2 10.4 %fusion.60 = f32[3072,768]{1,0:T(8,128)} fusion(bf16[1024,3072]{1,0:T(8,128)(2,1)} %get-tuple-element.371, bf16[1,1024,768]{2,1,0:T(8,128)(2,1)} %param.22), kind=kOutput, calls=%fused_computation.104 | convolution fusion | flops 4831838208 | bytes 17301504 | tf_op jit(solution)/shard_map/tf,td->fd/dot_general | solution.py:156
  539.1 10.4 %fusion.71 = bf16[1,1024,768]{1,2,0:T(8,128)(2,1)} fusion(f32[1024,768]{0,1:T(8,128)} %copy-done.10, f32[768]{0:T(1024)S(1)} %convert_element_type.191, bf16[1024,3072]{1,0:T(8,128)(2,1)} %get-tuple-element.371, bf16[3072,768]{1,0:T(8,128)(2,1)} %all-gather.12.cloned.1.call-done), kind=kOutput, calls=%fused_computation.115 | convolution fusion | flops 4834197504 | bytes 15731712 | tf_op jit(solution)/shard_map/dot_general | solution.py:143
  549.6 2.6 copy.73
  552.2 8.7 fusion.83
  560.9 3.7 copy.70
  564.6 3.2 fusion.49
  568.1 1.6 fusion.47
  570.5 3.2 convert_reduce_fusion.2
  573.7 40.3 %all-reduce.26 = (bf16[768]{0:T(1024)(128)(2,1)S(1)}, bf16[768]{0:T(1024)(128)(2,1)S(1)}, bf16[768]{0:T(1024)(128)(2,1)S(1)}, bf16[768]{0:T(1024)(128)(2,1)S(1)}...) all-reduce(f32[768]{0:T(1024)S(1)} %get-tuple-element.299, ...), channel_id=2, replica_groups=mesh['fsdp'=8,'dp'=4] {'fsdp','dp'}, use_global_device_ids=true, to_apply=%region_16.17.clone | all-reduce | flops 9216 | bytes 55296
  616.7 7.0 all-reduce.28
  628.4 3.6 copy.74
  632.8 5.4 all_gather.100
  640.0 6.8 all_gather.97
  647.8 127.2 %reduce-scatter.9.cloned.1.call-done = f32[24,3072]{1,0:T(8,128)} async-done(((f32[768,3072]{1,0:T(8,128)}), f32[24,3072]{1,0:T(8,128)}) %reduce-scatter.9.cloned.1.call-update) | async-done | bytes 294928 | tf_op jit(solution)/shard_map/reduce_scatter | solution.py:247
  775.9 7.5 all_gather.104
  784.5 131.7 %reduce-scatter.11.cloned.1.call-done = f32[96,768]{1,0:T(8,128)} async-done(((f32[3072,768]{1,0:T(8,128)}), f32[96,768]{1,0:T(8,128)}) %reduce-scatter.11.cloned.1.call-update) | async-done | bytes 294928 | tf_op jit(solution)/shard_map/reduce_scatter | solution.py:249
  917.2 7.5 all_gather.106
  (248 shorter events, 47.4 us)
Async XLA Ops:
  7.2 88.3 %all-gather.6.cloned.1.call-start = ((), (), s32[]{:S(2)}) async-start(), calls=%async_computation.4 | async-start | bytes 3981312 | tf_op jit(solution)/shard_map/all_gather | solution.py:76
  7.9 199.1 %all-gather.8.cloned.1.call-start = ((), (), s32[]{:S(2)}) async-start(), calls=%async_computation.5 | async-start | bytes 1327104 | tf_op jit(solution)/shard_map/all_gather | solution.py:79
  8.7 203.0 %all-gather.10.cloned.1.call-start = ((), (), s32[]{:S(2)}) async-start(), calls=%async_computation.6 | async-start | bytes 5308416 | tf_op jit(solution)/shard_map/all_gather | solution.py:83
  9.4 270.9 %all-gather.12.cloned.1.call-start = ((), (), s32[]{:S(2)}) async-start(), calls=%async_computation.7 | async-start | bytes 5308416 | tf_op jit(solution)/shard_map/all_gather | solution.py:85
  10.0 622.0 %reduce-scatter.7.cloned.1.call-start = ((), (), s32[]{:S(2)}) async-start(), calls=%async_computation.9 | async-start | bytes 2433024 | tf_op jit(solution)/shard_map/reduce_scatter | solution.py:243
  61.3 34.2 %copy-start.29 = (f32[768]{0:T(1024)}, f32[768]{0:T(1024)S(1)}, u32[]{:S(2)}) copy-start(f32[768]{0:T(1024)S(1)} %convert_element_type.177) | copy-start | bytes 9220
  61.9 33.6 %copy-start.49 = (f32[768]{0:T(1024)}, f32[768]{0:T(1024)S(1)}, u32[]{:S(2)}) copy-start(f32[768]{0:T(1024)S(1)} %convert_element_type.178) | copy-start | bytes 9220
  90.5 3.2 copy-start.17
  92.3 3.2 copy-start.7
  92.6 10.8 %copy-start.27 = (f32[1024]{0:T(1024)}, f32[1024]{0:T(1024)S(1)}, u32[]{:S(2)}) copy-start(f32[1024]{0:T(1024)S(1)} %broadcast_multiply_fusion.1) | copy-start | bytes 12292
  93.7 9.7 %copy-start.35 = (f32[1024]{0:T(1024)}, f32[1024]{0:T(1024)S(1)}, u32[]{:S(2)}) copy-start(f32[1024]{0:T(1024)S(1)} %fusion.73) | copy-start | bytes 12292
  116.7 3.1 copy-start.21
  120.1 23.4 %copy-start.6 = (bf16[1024,12,64]{0,2,1:T(8,128)(2,1)S(1)}, bf16[1024,12,64]{0,2,1:T(8,128)(2,1)}, u32[]{:S(2)}) copy-start(bf16[1024,12,64]{0,2,1:T(8,128)(2,1)} %get-tuple-element.541) | copy-start | bytes 4718596 | tf_op jit(solution)/shard_map/while/body/eval_jaxpr/while
  131.1 15.6 %copy-start = (f32[12,512,1024]{2,1,0:T(8,128)S(1)}, f32[12,512,1024]{2,1,0:T(8,128)}, u32[]{:S(2)}) copy-start(f32[12,512,1024]{2,1,0:T(8,128)} %get-tuple-element.501) | copy-start | bytes 75497472 | tf_op jit(solution)/shard_map/while/body/eval_jaxpr/while
  155.6 23.1 %copy-start.6 = (bf16[1024,12,64]{0,2,1:T(8,128)(2,1)S(1)}, bf16[1024,12,64]{0,2,1:T(8,128)(2,1)}, u32[]{:S(2)}) copy-start(bf16[1024,12,64]{0,2,1:T(8,128)(2,1)} %get-tuple-element.541) | copy-start | bytes 4718596 | tf_op jit(solution)/shard_map/while/body/eval_jaxpr/while
  166.3 15.5 %copy-start = (f32[12,512,1024]{2,1,0:T(8,128)S(1)}, f32[12,512,1024]{2,1,0:T(8,128)}, u32[]{:S(2)}) copy-start(f32[12,512,1024]{2,1,0:T(8,128)} %get-tuple-element.501) | copy-start | bytes 75497472 | tf_op jit(solution)/shard_map/while/body/eval_jaxpr/while
  201.2 5.8 copy-start.1
  201.2 5.8 copy-start.4
  201.2 5.8 copy-start.23
  201.2 5.8 copy-start.25
  201.2 5.8 copy-start.51
  211.2 105.7 %copy-start.10 = (f32[1024,768]{0,1:T(8,128)}, f32[1024,768]{0,1:T(8,128)S(1)}, u32[]{:S(2)}) copy-start(f32[1024,768]{0,1:T(8,128)S(1)} %get-tuple-element.383) | copy-start | bytes 9437188
  211.2 0.8 copy-start.45
  211.2 0.8 copy-start.47
  211.2 105.6 %copy-start.31 = (f32[1024]{0:T(1024)}, f32[1024]{0:T(1024)S(1)}, u32[]{:S(2)}) copy-start(f32[1024]{0:T(1024)S(1)} %broadcast_multiply_fusion) | copy-start | bytes 12292
  211.7 105.2 %copy-start.41 = (f32[1024]{0:T(1024)}, f32[1024]{0:T(1024)S(1)}, u32[]{:S(2)}) copy-start(f32[1024]{0:T(1024)S(1)} %fusion.74) | copy-start | bytes 12292
  313.4 3.5 copy-start.13
  316.9 1.4 copy-start.15
  317.8 1.7 copy-start.11
  317.8 1.7 copy-start.33
  318.3 2.0 copy-start.18
  327.8 2.9 copy-start.2
  327.8 2.9 copy-start.22
  327.8 2.9 copy-start.24
  327.8 2.9 copy-start.26
  329.4 309.6 %reduce-scatter.5.cloned.1.call-start = ((), (), s32[]{:S(2)}) async-start(), calls=%async_computation.8 | async-start | bytes 7299072 | tf_op jit(solution)/shard_map/reduce_scatter | solution.py:240
  331.3 11.7 %copy-start.14 = (bf16[2,512,12,64]{1,3,2,0:T(8,128)(2,1)S(1)}, bf16[2,512,12,64]{1,3,2,0:T(8,128)(2,1)}, u32[]{:S(2)}) copy-start(bf16[2,512,12,64]{1,3,2,0:T(8,128)(2,1)} %get-tuple-element.578) | copy-start | bytes 4718596 | tf_op jit(solution)/shard_map/while/body/eval_jaxpr/while
  397.0 9.5 %copy-start.5 = (bf16[2,512,12,64]{1,3,2,0:T(8,128)(2,1)S(1)}, bf16[2,512,12,64]{1,3,2,0:T(8,128)(2,1)}, u32[]{:S(2)}) copy-start(bf16[2,512,12,64]{1,3,2,0:T(8,128)(2,1)} %get-tuple-element.573) | copy-start | bytes 4718596 | tf_op jit(solution)/shard_map/while/body/eval_jaxpr/while
  415.5 11.5 %copy-start.14 = (bf16[2,512,12,64]{1,3,2,0:T(8,128)(2,1)S(1)}, bf16[2,512,12,64]{1,3,2,0:T(8,128)(2,1)}, u32[]{:S(2)}) copy-start(bf16[2,512,12,64]{1,3,2,0:T(8,128)(2,1)} %get-tuple-element.578) | copy-start | bytes 4718596 | tf_op jit(solution)/shard_map/while/body/eval_jaxpr/while
  480.7 9.5 %copy-start.5 = (bf16[2,512,12,64]{1,3,2,0:T(8,128)(2,1)S(1)}, bf16[2,512,12,64]{1,3,2,0:T(8,128)(2,1)}, u32[]{:S(2)}) copy-start(bf16[2,512,12,64]{1,3,2,0:T(8,128)(2,1)} %get-tuple-element.573) | copy-start | bytes 4718596 | tf_op jit(solution)/shard_map/while/body/eval_jaxpr/while
  499.9 3.6 copy-start.3
  503.8 2.8 copy-start.19
  503.8 4.0 copy-start.8
  503.8 4.0 copy-start.28
  503.8 4.0 copy-start.30
  503.8 4.0 copy-start.36
  503.8 4.0 copy-start.50
  506.5 1.2 copy-start.20
  514.8 0.7 copy-start.32
  514.8 0.7 copy-start.40
  514.8 0.7 copy-start.42
  514.8 0.7 copy-start.48
  514.8 260.1 %reduce-scatter.9.cloned.1.call-start = ((), (), s32[]{:S(2)}) async-start(), calls=%async_computation.10 | async-start | bytes 9732096 | tf_op jit(solution)/shard_map/reduce_scatter | solution.py:247
  526.1 390.1 %reduce-scatter.11.cloned.1.call-start = ((), (), s32[]{:S(2)}) async-start(), calls=%async_computation.11 | async-start | bytes 9732096 | tf_op jit(solution)/shard_map/reduce_scatter | solution.py:249
  536.6 2.5 copy-start.53
  564.5 3.2 copy-start.38
  564.5 3.6 copy-start.9
  568.1 1.9 copy-start.12
  568.1 2.4 copy-start.16
  568.1 2.4 copy-start.34
  570.5 3.3 copy-start.43
  570.5 3.3 copy-start.44
  570.5 3.3 copy-start.46
  570.5 3.3 copy-start.52
  (3 other events, 1.9 us)
Sparse Core Ops, SparseCore 0:
  10.2 67.9 all-gather.5
  80.3 39.9 all-gather.7
  122.5 78.0 all-gather.9
  202.6 77.6 all-gather.11
  329.5 98.0 reduce-scatter.6
  514.9 118.9 reduce-scatter.4
  639.8 135.0 reduce-scatter.8
  780.8 135.3 reduce-scatter.10
where the time goes:
time: 936 us; the launch traced here: 933 us
  matrix products  296 us (32%)
  waiting for transfers between devices  292 us (31%)
  blocking collectives  141 us (15%)
  other arithmetic  103 us (11%)
  local copies, waits for them, and re-layouts  71.9 us (8%)
  between operations  17 us (2%)
  loops' own time  11.4 us (1%)
    reduce_scatter x1, waiting for transfers between devices, per_device(): lax.psum_scatter(grad_fc2_weight, ('fsdp', 'dp'), scatter_dimension=0, ti...  132 us
    reduce_scatter x1, waiting for transfers between devices, per_device(): lax.psum_scatter(grad_fc1_weight, ('fsdp', 'dp'), scatter_dimension=0, ti...  127 us
    unnamed x3, blocking collectives  87.3 us
    dot_general x4, matrix products, masked_scores(): jnp.einsum('qhd,khd->hqk', query_part, key_row, preferred_element_type=jn...  44.8 us
    convert_element_type x2, other arithmetic, back_block(): score_grad = (probs * (prob_grad - jnp.sum(prob_grad * probs, axis=-1, ke...  43.2 us
    dot_general x1, matrix products, per_device(): jnp.dot(normed_two, whole_fc1, preferred_element_type=jnp.float32)  37.9 us
    dot_general x2, matrix products, back_block(): jnp.einsum('qhd,khd->hqk', dctx_part, value_row, preferred_element_type=j...  36.4 us
    unnamed x156, local copies, waits for them, and re-layouts  31.5 us
  transfers between devices with their start and end apart: 8, of which 3 were waited for; matrix products, arithmetic and copies ran while one was open for 44% of the time, Pallas kernels for 0%

commit v1 on v0

v1 whole, which is shorter than its diff:
```python
import jax
import jax.numpy as jnp
from jax import lax
from jax.sharding import PartitionSpec as P
from jax.experimental import pallas as pl
from jax.experimental.pallas import tpu as pltpu

HEADS = 12
HD = 64
SEG_MAX = 49
masked_fill = -1e30
PAIR = 2 * HD
QB = 128
WIN = 256


def dotf(a, b, ca, cb):
    return lax.dot_general(a, b, (((ca,), (cb,)), ((), ())), preferred_element_type=jnp.float32)


def window_start(i, seq):
    return min(max(i * QB - (WIN - QB) // 2, 0), seq - WIN)


def stack_heads(v):
    lane = lax.broadcasted_iota(jnp.int32, v.shape, 1)
    zero = jnp.zeros_like(v)
    return jnp.concatenate([jnp.where(lane < HD, v, zero), jnp.where(lane < HD, zero, v)], axis=0)


def fill_bias(seg_row, seg_col, bias_s, seq):
    for i in range(seq // QB):
        s = window_start(i, seq)
        same = seg_col[s : s + WIN, :] == seg_row[:, i * QB : (i + 1) * QB]
        bias_s[i] = jnp.where(same, 0.0, masked_fill)


def pick_heads(t):
    return jnp.concatenate([t[:HD, :QB], t[HD:, QB:]], axis=0)


def attend_kernel(seg_row, seg_col, q_ref, k_ref, v_ref, ctx_ref, lse_ref, bias_s):
    seq = q_ref.shape[0]

    @pl.when(pl.program_id(0) == 0)
    def _():
        fill_bias(seg_row, seg_col, bias_s, seq)

    for i in range(seq // QB):
        s = window_start(i, seq)
        rows = slice(i * QB, (i + 1) * QB)
        keys = k_ref[s : s + WIN, :]
        values = v_ref[s : s + WIN, :]
        q_st = stack_heads(q_ref[rows, :] * jnp.bfloat16(HD**-0.5))
        st = dotf(keys, q_st, 1, 1)
        bias = bias_s[i]
        st = jnp.concatenate([st[:, :QB] + bias, st[:, QB:] + bias], axis=1)
        top = jnp.max(st, axis=0, keepdims=True)
        p = jnp.exp(st - top)
        total = jnp.sum(p, axis=0, keepdims=True)
        ctx_t = dotf(values, p.astype(jnp.bfloat16), 0, 0) * (1.0 / total)
        ctx_ref[rows, :] = jnp.transpose(pick_heads(ctx_t)).astype(jnp.bfloat16)
        lse = top + jnp.log(total)
        lse_ref[0, 0:1, rows] = lse[:, :QB]
        lse_ref[0, 1:2, rows] = lse[:, QB:]


def attend_back_kernel(
    seg_row, seg_col, q_ref, k_ref, v_ref, dctx_ref, lse_ref, dqkv_ref, colsum_ref, bias_s, dk_s, dv_s
):
    seq = q_ref.shape[0]

    @pl.when(pl.program_id(0) == 0)
    def _():
        fill_bias(seg_row, seg_col, bias_s, seq)

    dk_s[...] = jnp.zeros_like(dk_s)
    dv_s[...] = jnp.zeros_like(dv_s)
    for i in range(seq // QB):
        s = window_start(i, seq)
        rows = slice(i * QB, (i + 1) * QB)
        win = slice(s, s + WIN)
        keys = k_ref[win, :]
        values = v_ref[win, :]
        q_st = stack_heads(q_ref[rows, :] * jnp.bfloat16(HD**-0.5))
        d_st = stack_heads(dctx_ref[rows, :])
        st = dotf(keys, q_st, 1, 1)
        bias = bias_s[i]
        lse_a = lse_ref[0, 0:1, rows]
        lse_b = lse_ref[0, 1:2, rows]
        st = jnp.concatenate([st[:, :QB] + bias - lse_a, st[:, QB:] + bias - lse_b], axis=1)
        p = jnp.exp(st)
        dp = dotf(values, d_st, 1, 1)
        ds = (p * (dp - jnp.sum(dp * p, axis=0, keepdims=True))).astype(jnp.bfloat16)
        dv_s[win, :] += dotf(p.astype(jnp.bfloat16), d_st, 1, 0)
        dk_s[win, :] += dotf(ds, q_st, 1, 0)
        dq_t = pick_heads(dotf(keys, ds, 0, 0)) * (HD**-0.5)
        dqkv_ref[0, rows, :] = jnp.transpose(dq_t).astype(jnp.bfloat16)
    dqkv_ref[1] = dk_s[...].astype(jnp.bfloat16)
    dqkv_ref[2] = dv_s[...].astype(jnp.bfloat16)
    for g in range(3):
        colsum_ref[g] = jnp.sum(dqkv_ref[g].astype(jnp.float32), axis=0, keepdims=True)


def attention(qkv, seg):
    seq = qkv.shape[0]
    pairs = HEADS // 2
    full = lambda *shape: pl.BlockSpec(shape, lambda h: (0,) * len(shape))
    col = lambda g: pl.BlockSpec((seq, PAIR), lambda h, g=g: (0, g * pairs + h))
    return pl.pallas_call(
        attend_kernel,
        grid=(pairs,),
        in_specs=[full(1, seq), full(seq, 1), col(0), col(1), col(2)],
        out_specs=[
            pl.BlockSpec((seq, PAIR), lambda h: (0, h)),
            pl.BlockSpec((1, 2, seq), lambda h: (h, 0, 0)),
        ],
        out_shape=[
            jax.ShapeDtypeStruct((seq, HEADS * HD), jnp.bfloat16),
            jax.ShapeDtypeStruct((pairs, 2, seq), jnp.float32),
        ],
        scratch_shapes=[pltpu.VMEM((seq // QB, WIN, QB), jnp.float32)],
        name="attend",
    )(seg.reshape(1, seq), seg.reshape(seq, 1), qkv, qkv, qkv)


def attention_back(qkv, seg, dctx, lse):
    seq = qkv.shape[0]
    pairs = HEADS // 2
    full = lambda *shape: pl.BlockSpec(shape, lambda h: (0,) * len(shape))
    col = lambda g: pl.BlockSpec((seq, PAIR), lambda h, g=g: (0, g * pairs + h))
    return pl.pallas_call(
        attend_back_kernel,
        grid=(pairs,),
        in_specs=[
            full(1, seq),
            full(seq, 1),
            col(0),
            col(1),
            col(2),
            pl.BlockSpec((seq, PAIR), lambda h: (0, h)),
            pl.BlockSpec((1, 2, seq), lambda h: (h, 0, 0)),
        ],
        out_specs=[
            pl.BlockSpec((3, seq, PAIR), lambda h: (0, 0, h)),
            pl.BlockSpec((3, 1, PAIR), lambda h: (0, 0, h)),
        ],
        out_shape=[
            jax.ShapeDtypeStruct((3, seq, HEADS * HD), jnp.bfloat16),
            jax.ShapeDtypeStruct((3, 1, HEADS * HD), jnp.float32),
        ],
        scratch_shapes=[
            pltpu.VMEM((seq // QB, WIN, QB), jnp.float32),
            pltpu.VMEM((seq, PAIR), jnp.float32),
            pltpu.VMEM((seq, PAIR), jnp.float32),
        ],
        name="attend_back",
    )(seg.reshape(1, seq), seg.reshape(seq, 1), qkv, qkv, qkv, dctx, lse)


epsilon = 1e-06
RING_MAX = 16


def ring_order(n):
    if n % 2:
        return list(range(n))
    return list(range(0, n, 2)) + list(range(n - 1, 0, -2))


def core_pairs(dp):
    return [(d, d ^ 1) for d in range(dp)]


def core_swap(v, dp):
    return lax.ppermute(v, "dp", core_pairs(dp))


def ring_gather(piece, n, dp):
    order = ring_order(n)
    place = {f: p for p, f in enumerate(order)}
    up = [(order[p], order[(p + 1) % n]) for p in range(n)]
    down = [(order[(p + 1) % n], order[p]) for p in range(n)]
    here = jnp.asarray([place[f] for f in range(n)], jnp.int32)[lax.axis_index("fsdp")]
    source = lambda shift: jnp.asarray(order, jnp.int32)[(here + shift) % n]
    pieces = [(piece, source(0))]
    right = left = piece
    for s in range(1, (n - 1) // 2 + 1):
        right = lax.ppermute(right, "fsdp", up)
        left = lax.ppermute(left, "fsdp", down)
        pieces += [(right, source(n - s)), (left, source(s))]
    if n % 2 == 0:
        half = n // 2
        if n > 2:
            last = jnp.where(lax.axis_index("dp") % 2 == 0, right, left)
        else:
            last = piece
        both = []
        for d in range(dp):
            both += [(a * dp + d, b * dp + d) for a, b in (up if d % 2 == 0 else down)]
        pieces.append((lax.ppermute(last, ("fsdp", "dp"), both), source(half)))
    return pieces


def assemble(pieces, others, table, moves, out_shapes):
    count = len(pieces)

    def kernel(table_ref, *refs):
        ins, rest = refs[: 2 * count], refs[2 * count :]
        outs, sems = rest[:-1], rest[-1]
        core = table_ref[count]
        copies = []
        for k in range(2 * count):
            where = table_ref[k % count]
            c = core if k < count else 1 - core
            for o, r0, rows, c0, cols, step, core_step, first, col in moves:
                if core_step == 0 and k >= count:
                    continue
                row = pl.multiple_of(where * step + c * core_step + first, 8)
                copy = pltpu.make_async_copy(
                    ins[k].at[pl.ds(r0, rows), pl.ds(c0, cols)],
                    outs[o].at[pl.ds(row, rows), pl.ds(col, cols)],
                    sems.at[len(copies)],
                )
                copy.start()
                copies.append(copy)
        for copy in copies:
            copy.wait()

    total = 2 * count * len(moves)
    any_space = pl.BlockSpec(memory_space=pl.ANY)
    return pl.pallas_call(
        kernel,
        grid_spec=pltpu.PrefetchScalarGridSpec(
            num_scalar_prefetch=1,
            grid=(),
            in_specs=[any_space] * (2 * count),
            out_specs=[any_space] * len(out_shapes),
            scratch_shapes=[pltpu.SemaphoreType.DMA((total,))],
        ),
        out_shape=[jax.ShapeDtypeStruct(s, jnp.bfloat16) for s in out_shapes],
        name="assemble",
    )(table, *pieces, *others)


def gather_group(piece, n, dp, moves, out_shapes):
    got = ring_gather(piece, n, dp)
    pieces = [p for p, _ in got]
    others = [core_swap(p, dp) for p in pieces]
    table = jnp.stack([f for _, f in got] + [lax.axis_index("dp") % 2]).astype(jnp.int32)
    return assemble(pieces, others, table, moves, out_shapes)


def take(v, i, axis):
    return lax.dynamic_index_in_dim(v, i, axis, keepdims=False)


def wide(v):
    return v.astype(jnp.float32)


def low(v):
    return v.astype(jnp.bfloat16)


def reduce_group(blocks, n, dp):
    _, rows, columns = blocks.shape
    half = columns // 2
    f = lax.axis_index("fsdp")
    d = lax.axis_index("dp")
    core = d % 2
    slab = lambda c: lax.dynamic_slice_in_dim(blocks, c * half, half, 2)
    both = wide(slab(core)) + wide(core_swap(slab(1 - core), dp))
    pair = both.reshape(n // 2, 2, rows, half)
    flip = [(i, i ^ 1) for i in range(n)]
    sent = lax.ppermute(low(take(pair, 1 - f % 2, 1)), "fsdp", flip)
    mine = take(pair, f % 2, 1) + wide(sent)
    z = f // 2
    total = take(mine, z, 0)
    for k in range(1, n // 2):
        hop = [(i, ((i // 2) ^ k) * 2 + i % 2) for i in range(n)]
        total = total + wide(lax.ppermute(low(take(mine, z ^ k, 0)), "fsdp", hop))
    total = low(total)
    if dp > 2:
        total = low(wide(total) + wide(lax.ppermute(total, "dp", [(i, i ^ 2) for i in range(dp)])))
    other = core_swap(total, dp)
    first = core == 0
    return jnp.concatenate([jnp.where(first, total, other), jnp.where(first, other, total)], axis=1)


def gelu_kernel(x_ref, w_ref, b_ref, act_ref, slope_ref):
    rows = 256
    for r in range(x_ref.shape[0] // rows):
        at = slice(r * rows, (r + 1) * rows)
        h = jnp.dot(x_ref[at, :], w_ref[...], preferred_element_type=jnp.float32) + b_ref[...]
        size = jnp.abs(h)
        t = 1.0 / (1.0 + (0.3275911 * 0.7071067811865476) * size)
        e = jnp.exp(-0.5 * h * h)
        poly = t * (
            0.5 * 0.254829592
            + t * (-0.5 * 0.284496736 + t * (0.5 * 1.421413741 + t * (-0.5 * 1.453152027 + t * (0.5 * 1.061405429))))
        )
        tail = poly * e
        upper = jnp.where(h >= 0.0, 1.0 - tail, tail)
        act_ref[at, :] = (h * upper).astype(jnp.bfloat16)
        slope_ref[at, :] = (upper + (h * 0.3989422804014327) * e).astype(jnp.bfloat16)


def gelu_layer(x, w, b):
    rows, width = x.shape
    ff = w.shape[1]
    tile = 512
    out = pl.BlockSpec((rows, tile), lambda j: (0, j))
    return pl.pallas_call(
        gelu_kernel,
        grid=(ff // tile,),
        in_specs=[
            pl.BlockSpec((rows, width), lambda j: (0, 0)),
            pl.BlockSpec((width, tile), lambda j: (0, j)),
            pl.BlockSpec((1, tile), lambda j: (0, j)),
        ],
        out_specs=[out, out],
        out_shape=[jax.ShapeDtypeStruct((rows, ff), jnp.bfloat16)] * 2,
        name="gelu_layer",
    )(x, w, b.reshape(1, ff))


def norm_parts(v):
    c = v - jnp.mean(v, axis=-1, keepdims=True)
    r = lax.rsqrt(jnp.mean(c * c, axis=-1, keepdims=True) + epsilon)
    return c * r, r


def norm_back(dn, x, r, gain):
    u = dn * gain
    e = r * (u - jnp.mean(u, axis=-1, keepdims=True) - x * jnp.mean(u * x, axis=-1, keepdims=True))
    return e, jnp.sum(dn * x, axis=0), jnp.sum(dn, axis=0)


def column_sum(v):
    return jnp.sum(v.astype(jnp.float32), axis=0)


def matmul(a, b, ca, cb):
    return lax.dot_general(a, b, (((ca,), (cb,)), ((), ())), preferred_element_type=jnp.float32)


def gather_all(shards, n, dp):
    qkv, proj, fc1, fc2, vectors = shards
    rows, wide_columns = qkv.shape
    width = proj.shape[1]
    ff = fc1.shape[1]
    if n > RING_MAX or dp != 4:
        gather = lambda v: lax.all_gather(v, "fsdp", axis=0, tiled=True)
        small = lax.all_gather(vectors, "fsdp", axis=0)
        return gather(qkv), gather(proj), gather(fc1), gather(fc2), small
    core = lax.axis_index("dp") % 2
    cut = lambda v: lax.dynamic_slice_in_dim(v, core * (v.shape[0] // 2), v.shape[0] // 2, 0)
    half = rows // 2
    top = jnp.concatenate([cut(qkv), cut(proj)], axis=1)
    extra = jnp.pad(vectors.reshape(1, -1), ((0, 7), (0, top.shape[1] - vectors.shape[0])))
    first = jnp.concatenate([top, extra], axis=0)
    wqkv, wproj, small = gather_group(
        first,
        n,
        dp,
        [
            (0, 0, half, 0, wide_columns, rows, half, 0, 0),
            (1, 0, half, wide_columns, width, rows, half, 0, 0),
            (2, half, 8, 0, top.shape[1], 8, 0, 0, 0),
        ],
        [(n * rows, wide_columns), (n * rows, width), (n * 8, top.shape[1])],
    )
    small = small.reshape(n, 8, -1)[:, 0, : vectors.shape[0]]
    parts = ff // width
    deep = cut(fc2).reshape(parts, half, width)
    second = jnp.concatenate([cut(fc1)] + [jnp.concatenate([deep[j] for j in range(parts)], axis=1)], axis=0)
    second, _ = lax.optimization_barrier((second, wproj))
    w1, w2 = gather_group(
        second,
        n,
        dp,
        [(0, 0, half, 0, ff, rows, half, 0, 0)]
        + [
            (1, half, half, j * width, width, rows * parts, half * parts, j * half, 0)
            for j in range(parts)
        ],
        [(n * rows, ff), (n * rows * parts, width)],
    )
    return wqkv, wproj, w1, w2, small


def reduce_all(blocks, n, dp):
    if n > RING_MAX or dp != 4:
        flat = blocks.reshape(n * blocks.shape[1], blocks.shape[2])
        return low(lax.psum(lax.psum_scatter(flat, "fsdp", scatter_dimension=0, tiled=True), "dp"))
    return reduce_group(blocks, n, dp)


def per_device(n, dp, tokens, segment_ids, cotangent, *params):
    (
        ln1_gain,
        ln1_bias,
        qkv_weight,
        query_bias,
        value_bias,
        proj_weight,
        proj_bias,
        ln2_gain,
        ln2_bias,
        fc1_weight,
        fc1_bias,
        fc2_weight,
        fc2_bias,
    ) = params
    _, seq, width = tokens.shape
    shard = ln1_gain.shape[0]
    ff = fc1_weight.shape[1]
    vectors = jnp.concatenate(
        [ln1_gain, ln1_bias, query_bias, value_bias, proj_bias, ln2_gain, ln2_bias, fc2_bias, fc1_bias]
    )
    wqkv, wproj, w1, w2, small = gather_all((qkv_weight, proj_weight, fc1_weight, fc2_weight, vectors), n, dp)
    small = wide(small)
    whole = [small[:, j * shard : (j + 1) * shard].reshape(-1) for j in range(8)]
    g1, b1, bq, bv, bp, g2, b2, b_fc2 = whole
    b_fc1 = small[:, 8 * shard :].reshape(-1)

    flat = wide(tokens.reshape(seq, width))
    seg = segment_ids.reshape(seq)
    x1, r1 = norm_parts(flat)
    n1 = low(x1 * g1 + b1)
    shift = jnp.concatenate([bq, jnp.zeros_like(bq), bv])
    qkv = low(matmul(n1, wqkv, 1, 0) + shift)
    ctx, lse = attention(qkv, seg)
    middle = flat + (matmul(ctx, wproj, 1, 0) + bp)
    x2, r2 = norm_parts(middle)
    n2 = low(x2 * g2 + b2)
    act, slope = gelu_layer(n2, w1, b_fc1)
    layer_out = low(middle + (matmul(act, w2, 1, 0) + b_fc2))

    d_branch = cotangent.reshape(seq, width)
    upstream = wide(d_branch)
    grad_fc2_bias = column_sum(d_branch)
    grad_fc2 = low(matmul(act, d_branch, 0, 0))
    out_fc2 = reduce_all(grad_fc2.reshape(n, ff // n, width), n, dp)
    d_hidden = low(matmul(d_branch, w2, 1, 1) * wide(slope))
    grad_fc1_bias = column_sum(d_hidden)
    grad_fc1 = low(matmul(n2, d_hidden, 0, 0))
    out_fc1 = reduce_all(grad_fc1.reshape(n, shard, ff), n, dp)
    d_norm_two = matmul(d_hidden, w1, 1, 1)
    e2, grad_ln2_gain, grad_ln2_bias = norm_back(d_norm_two, x2, r2, g2)
    d_middle = upstream + e2
    d_attn = low(d_middle)
    grad_proj_bias = column_sum(d_attn)
    grad_proj = low(matmul(ctx, d_attn, 0, 0))
    d_ctx = low(matmul(d_attn, wproj, 1, 1))
    d_qkv, sums = attention_back(qkv, seg, d_ctx, lse)
    grads = [low(matmul(n1, d_qkv[g], 0, 0)) for g in range(3)]
    d_norm_one = sum(matmul(d_qkv[g], wqkv[:, g * width : (g + 1) * width], 1, 1) for g in range(3))
    e1, grad_ln1_gain, grad_ln1_bias = norm_back(d_norm_one, x1, r1, g1)
    input_grad = d_middle + e1

    top = jnp.concatenate(grads + [grad_proj], axis=1).reshape(n, shard, 4 * width)
    tiny = jnp.stack(
        [
            grad_ln1_gain,
            grad_ln1_bias,
            sums[0, 0],
            sums[2, 0],
            grad_proj_bias,
            grad_ln2_gain,
            grad_ln2_bias,
            grad_fc2_bias,
        ]
    ).reshape(8, n, shard)
    tiny = jnp.concatenate([tiny.transpose(1, 0, 2).reshape(n, -1), grad_fc1_bias.reshape(n, -1)], axis=1)
    tiny = jnp.pad(low(tiny)[:, None, :], ((0, 0), (0, 7), (0, 4 * width - tiny.shape[1])))
    out_last = reduce_all(jnp.concatenate([top, tiny], axis=1), n, dp)
    out_last = wide(out_last)
    line = out_last[shard]
    vec = [line[j * shard : (j + 1) * shard] for j in range(8)]
    return (
        layer_out.reshape(tokens.shape),
        input_grad.reshape(tokens.shape),
        vec[0],
        vec[1],
        out_last[:shard, : 3 * width],
        vec[2],
        vec[3],
        out_last[:shard, 3 * width :],
        vec[4],
        vec[5],
        vec[6],
        wide(out_fc1),
        line[8 * shard : 8 * shard + ff // n],
        wide(out_fc2),
        vec[7],
    )


def solution(mesh):
    n, dp = mesh.shape["fsdp"], mesh.shape["dp"]
    rows = P(("fsdp", "dp"), None, None)
    vec, mat = P("fsdp"), P("fsdp", None)
    params = (vec, vec, mat, vec, vec, mat, vec, vec, vec, mat, vec, mat, vec)
    return jax.shard_map(
        lambda *args: per_device(n, dp, *args),
        mesh=mesh,
        in_specs=(rows, P(("fsdp", "dp"), None), rows) + params,
        out_specs=(rows, rows) + params,
        check_vma=False,
    )
```

time: 936 us -> 839 us (0.90)
  Pallas kernels: 0 us -> 500 us
  matrix products: 296 us -> 76.2 us
  waiting for transfers between devices: 292 us -> 136 us
  blocking collectives: 141 us -> 0 us
  other arithmetic: 103 us -> 27.8 us
  starting transfers between devices: 0.31 us -> 41.7 us
  local copies, waits for them, and re-layouts: 71.9 us -> 41.4 us
  loops' own time: 11.4 us -> 0 us
    pallas_call x0 -> x5, Pallas kernels: none -> 500 us  [the longest x2 445 us: assemble(): pl.pallas_call(kernel, grid_spec=pltpu.PrefetchScalarGridSpec(num_scalar_...]
    reduce_scatter x4 -> x0, waiting for transfers between devices: 259 us -> none  [the longest x1 132 us: per_device(): lax.psum_scatter(grad_fc2_weight, ('fsdp', 'dp'), scatter_dimension=0, ti...]
    dot_general x26 -> x15, matrix products: 296 us -> 76.2 us  [matmul(): lax.dot_general(a, b, (((ca,), (cb,)), ((), ())), preferred_element_type=...]
    ppermute x0 -> x51, waiting for transfers between devices: none -> 136 us  [the longest x3 43.7 us: reduce_group(): sent = lax.ppermute(low(take(pair, 1 - f % 2, 1)), 'fsdp', flip)]
    unnamed x3 -> x0, blocking collectives: 87.3 us -> none
    all_gather x5 -> x0, blocking collectives: 54.2 us -> none  [the longest x1 26.8 us: per_device(): lax.all_gather(fc1_bias, 'fsdp', axis=0, tiled=True)]
    convert_element_type x28 -> x11, other arithmetic: 58 us -> 6.65 us  [the longest x7 4.32 us: low(): return v.astype(jnp.bfloat16)]
    ppermute x0 -> x51, starting transfers between devices: none -> 41.7 us  [the longest x9 12 us: reduce_group(): total = total + wide(lax.ppermute(low(take(mine, z ^ k, 0)), 'fsdp', hop))]
  transfers between devices with their start and end apart: 8 -> 51, of which waited for: 3 -> 19; matrix products, arithmetic and copies ran while one was open for 44% -> 8% of each run, Pallas kernels for 0% -> 2%
where the time goes in v1:
time: 839 us; the launch traced here: 832 us
  Pallas kernels  500 us (60%)
  waiting for transfers between devices  136 us (16%)
  matrix products  76.2 us (9%)
  starting transfers between devices  41.7 us (5%)
  local copies, waits for them, and re-layouts  41.4 us (5%)
  other arithmetic  27.8 us (3%)
  between operations  8.63 us (1%)
    pallas_call x2, Pallas kernels, assemble(): pl.pallas_call(kernel, grid_spec=pltpu.PrefetchScalarGridSpec(num_scalar_...  445 us
    dot_general x15, matrix products, matmul(): lax.dot_general(a, b, (((ca,), (cb,)), ((), ())), preferred_element_type=...  76.2 us
    ppermute x3, waiting for transfers between devices, reduce_group(): sent = lax.ppermute(low(take(pair, 1 - f % 2, 1)), 'fsdp', flip)  43.7 us
    ppermute x9, waiting for transfers between devices, reduce_group(): total = total + wide(lax.ppermute(low(take(mine, z ^ k, 0)), 'fsdp', hop))  43.3 us
    ppermute x6, waiting for transfers between devices, ring_gather(): left = lax.ppermute(left, 'fsdp', down)  39.4 us
    pallas_call x1, Pallas kernels, attention_back(): pl.pallas_call(attend_back_kernel, grid=(pairs,), in_specs=[full(1, seq),...  19 us
    pallas_call x1, Pallas kernels, attention(): pl.pallas_call(attend_kernel, grid=(pairs,), in_specs=[full(1, seq), full...  17.9 us
    pallas_call x1, Pallas kernels, gelu_layer(): pl.pallas_call(gelu_kernel, grid=(ff // tile,), in_specs=[pl.BlockSpec((r...  17.8 us
  transfers between devices with their start and end apart: 51, of which 19 were waited for; matrix products, arithmetic and copies ran while one was open for 8% of the time, Pallas kernels for 2%

profile of v1, /device:TPU:0, one launch (start us, length us, event | category | flops | bytes accessed | tf_op | source)
XLA Modules:
  0.0 831.8 jit_solution(14181988201187365318)
XLA Ops:
  0.7 6.2 concatenate.51
  8.9 3.0 collective-permute-start.1
  12.0 8.1 collective-permute-done.1.refs_2_
  20.1 1.7 collective-permute-start.3
  22.2 7.4 collective-permute-done.3.refs_4_
  29.6 1.4 collective-permute-start.5
  39.5 1.7 reduce.2
  42.9 1.7 constant_dynamic-slice_fusion.2
  45.6 1.5 collective-permute-start.6
  47.1 5.8 stack.36.table_ref
  58.1 157.1 %assemble.2 = (bf16[768,2304]{1,0:T(8,128)(2,1)}, bf16[768,768]{1,0:T(8,128)(2,1)}, bf16[64,3072]{1,0:T(8,128)(2,1)}) custom-call(s32[9]{0:T(128)} %stack.36.table_ref, bf16[56,3072]{1,0:T(8,128)(2,1)} %copy-done.17, bf16[56,3072]{1,0:T(8,128)(2,1)} %collective-permute-done.refs_1_, bf16[56,3072]{1,0:T(8,128)(2,1)} %collective-permute-done.1.refs_2_, ...), custom_call_target="tpu_custom_call" | custom-call | tf_op jit(solution)/shard_map/assemble/pallas_call | solution.py:232
  215.2 1.4 collective-permute-start.16
  218.9 11.7 %collective-permute-done.16.refs_2_ = bf16[96,3072]{1,0:T(8,128)(2,1)S(1)} collective-permute-done((bf16[96,3072]{1,0:T(8,128)(2,1)S(1)}, bf16[96,3072]{1,0:T(8,128)(2,1)S(1)}, u32[]{:S(2)}, u32[]{:S(2)}) %collective-permute-start.16) | collective-permute-done | bytes 589856 | tf_op jit(solution)/shard_map/ppermute | solution.py:190
  230.6 1.5 collective-permute-start.18
  233.1 12.1 %collective-permute-done.18.refs_4_ = bf16[96,3072]{1,0:T(8,128)(2,1)} collective-permute-done((bf16[96,3072]{1,0:T(8,128)(2,1)S(1)}, bf16[96,3072]{1,0:T(8,128)(2,1)}, u32[]{:S(2)}, u32[]{:S(2)}) %collective-permute-start.18) | collective-permute-done | bytes 589856 | tf_op jit(solution)/shard_map/ppermute | solution.py:190
  245.3 1.7 collective-permute-start.20
  247.3 7.9 add_convert_fusion.q_ref.k_ref.v_ref
  255.2 17.9 %attend.1 = (bf16[1024,768]{1,0:T(8,128)(2,1)}, f32[6,2,1024]{2,1,0:T(2,128)}) custom-call(s32[1,1024]{1,0:T(1,128)} %seg_row.3, s32[1024,1]{1,0:T(8,128)} %copy.61.seg_col, bf16[1024,2304]{1,0:T(8,128)(2,1)} %add_convert_fusion.q_ref.k_ref.v_ref, bf16[1024,2304]{1,0:T(8,128)(2,1)} %add_convert_fusion.q_ref.k_ref.v_ref, ...), custom_call_target="tpu_custom_call" | custom-call | tf_op jit(solution)/shard_map/attend/pallas_call | solution.py:110
  273.6 2.1 collective-permute-start.21
  275.7 3.3 fusion.102
  279.1 1.6 copy-done.2
  282.6 1.5 collective-permute-done.21.refs_7_
  285.0 3.6 add_convert_fusion.2.x_ref
  289.4 288.4 %assemble.3 = (bf16[768,3072]{1,0:T(8,128)(2,1)}, bf16[3072,768]{1,0:T(8,128)(2,1)}) custom-call(s32[9]{0:T(128)} %stack.36.table_ref, bf16[96,3072]{1,0:T(8,128)(2,1)} %copy-done.12, bf16[96,3072]{1,0:T(8,128)(2,1)} %copy-done.19, bf16[96,3072]{1,0:T(8,128)(2,1)} %copy-done.18, bf16[96,3072]{1,0:T(8,128)(2,1)} %collective-permute-done.17.refs_3_, ...), custom_call_target="tpu_custom_call" | custom-call | tf_op jit(solution)/shard_map/assemble/pallas_call | solution.py:232
  577.8 17.8 %gelu_layer.1 = (bf16[1024,3072]{1,0:T(8,128)(2,1)}, bf16[1024,3072]{1,0:T(8,128)(2,1)}) custom-call(bf16[1024,768]{1,0:T(8,128)(2,1)} %add_convert_fusion.2.x_ref, bf16[768,3072]{1,0:T(8,128)(2,1)} %get-tuple-element.32.w_ref, f32[1,3072]{1,0:T(1,128)} %bitcast.207), custom_call_target="tpu_custom_call" | custom-call | tf_op jit(solution)/shard_map/gelu_layer/pallas_call | solution.py:314
  595.6 9.2 %fusion.103 = (bf16[3072]{0:T(1024)(128)(2,1)S(1)}, bf16[1024,3072]{1,0:T(8,128)(2,1)S(1)}) fusion(bf16[1024,3072]{1,0:T(8,128)(2,1)} %get-tuple-element.35, bf16[3072,768]{1,0:T(8,128)(2,1)} %get-tuple-element.34, bf16[1,1024,768]{2,1,0:T(8,128)(2,1)} %param.36), kind=kOutput, calls=%fused_computation.194 | convolution fusion | flops 4844418048 | bytes 18880512 | tf_op jit(solution)/shard_map/dot_general | solution.py:345
  604.9 5.7 multiply_reduce_fusion
  612.0 1.5 convolution_convert_fusion.3
  614.2 2.6 convolution_convert_fusion.2.dctx_ref
  616.8 19.0 %attend_back.1 = (bf16[3,1024,768]{2,1,0:T(8,128)(2,1)}, f32[3,1,768]{2,1,0:T(1,128)}) custom-call(s32[1,1024]{1,0:T(1,128)} %seg_row.3, s32[1024,1]{1,0:T(8,128)} %copy.61.seg_col, bf16[1024,2304]{1,0:T(8,128)(2,1)} %add_convert_fusion.q_ref.k_ref.v_ref, bf16[1024,2304]{1,0:T(8,128)(2,1)} %add_convert_fusion.q_ref.k_ref.v_ref, ...), custom_call_target="tpu_custom_call" | custom-call | tf_op jit(solution)/shard_map/attend_back/pallas_call | solution.py:132
  635.8 4.3 fusion.44
  640.1 2.8 fusion.47
  643.0 2.8 fusion.50
  645.8 3.0 fusion.32
  648.8 3.2 fusion.36
  652.0 7.1 convolution_convert_fusion.1
  659.2 6.9 convolution_convert_fusion
  666.6 5.0 pad_maximum_fusion
  671.6 6.6 copy.64
  678.2 3.5 constant_dynamic-slice_fusion.6
  682.1 6.7 fusion.16
  689.3 2.0 fusion.22
  691.5 2.0 constant_dynamic-slice_fusion.5
  694.3 9.1 %fusion.55 = bf16[1,1024,768]{2,1,0:T(8,128)(2,1)} fusion(f32[1024,768]{1,0:T(8,128)S(1)} %copy-done.4, f32[768]{0:T(1024)S(1)} %add.432, bf16[1024,3072]{1,0:T(8,128)(2,1)} %get-tuple-element.33, bf16[3072,768]{1,0:T(8,128)(2,1)S(1)} %bitcast.214), kind=kOutput, calls=%fused_computation.79 | convolution fusion | flops 4834197504 | bytes 15731712 | tf_op jit(solution)/shard_map/dot_general | solution.py:345
  703.4 2.2 convert_add_fusion.1
  705.8 1.7 collective-permute-start.45
  710.0 1.7 collective-permute-start.31
  711.8 22.9 %collective-permute-done.45 = bf16[4,384,384]{2,1,0:T(8,128)(2,1)S(1)} collective-permute-done((bf16[4,384,384]{2,1,0:T(8,128)(2,1)S(1)}, bf16[4,384,384]{2,1,0:T(8,128)(2,1)S(1)}, u32[]{:S(2)}, u32[]{:S(2)}) %collective-permute-start.45) | collective-permute-done | bytes 1179680 | tf_op jit(solution)/shard_map/ppermute | solution.py:276
  735.0 1.6 collective-permute-start.46
  736.7 2.5 collective-permute-start.48
  739.2 20.8 %collective-permute-done.38 = bf16[4,96,1536]{2,1,0:T(8,128)(2,1)S(1)} collective-permute-done((bf16[4,96,1536]{2,1,0:T(8,128)(2,1)S(1)}, bf16[4,96,1536]{2,1,0:T(8,128)(2,1)S(1)}, u32[]{:S(2)}, u32[]{:S(2)}) %collective-permute-start.38) | collective-permute-done | bytes 1179680 | tf_op jit(solution)/shard_map/ppermute | solution.py:276
  760.4 1.6 collective-permute-start.39
  762.1 2.5 collective-permute-start.41
  764.7 2.4 fusion.15
  767.2 1.6 collective-permute-start.49
  768.8 7.0 collective-permute-done.39
  775.8 3.1 collective-permute-done.41
  778.8 9.8 %collective-permute-done.40 = bf16[96,1536]{1,0:T(8,128)(2,1)S(1)} collective-permute-done((bf16[96,1536]{1,0:T(8,128)(2,1)S(1)}, bf16[96,1536]{1,0:T(8,128)(2,1)S(1)}, u32[]{:S(2)}, u32[]{:S(2)}) %collective-permute-start.40) | collective-permute-done | bytes 294944 | tf_op jit(solution)/shard_map/ppermute | solution.py:282
  788.8 1.5 collective-permute-start.42
  790.9 2.7 collective-permute-start.34
  795.7 8.2 collective-permute-done.32
  803.9 4.7 collective-permute-done.34
  808.7 10.5 %collective-permute-done.33 = bf16[104,1536]{1,0:T(8,128)(2,1)S(1)} collective-permute-done((bf16[104,1536]{1,0:T(8,128)(2,1)S(1)}, bf16[104,1536]{1,0:T(8,128)(2,1)S(1)}, u32[]{:S(2)}, u32[]{:S(2)}) %collective-permute-start.33) | collective-permute-done | bytes 319520 | tf_op jit(solution)/shard_map/ppermute | solution.py:282
  821.2 5.2 collective-permute-done.35
  (267 shorter events, 37.6 us)
Async XLA Ops:
  0.6 52.2 %copy-start = (bf16[96,3072]{1,0:T(8,128)(2,1)S(1)}, bf16[96,3072]{1,0:T(8,128)(2,1)}, u32[]{:S(2)}) copy-start(bf16[96,3072]{1,0:T(8,128)(2,1)} %param.46) | copy-start | bytes 1769476
  0.7 41.6 %copy-start.30 = (s32[8]{0:T(128)S(1)}, s32[8]{0:T(128)}, u32[]{:S(2)}) copy-start(s32[8]{0:T(128)} %constant.231.clone) | copy-start | bytes 100
  0.7 40.6 %copy-start.29 = (s32[1,1024]{1,0:T(1,128)S(1)}, s32[1,1024]{1,0:T(1,128)}, u32[]{:S(2)}) copy-start(s32[1,1024]{1,0:T(1,128)} %seg_row.3) | copy-start | bytes 12292
  0.7 43.9 %copy-start.5 = (bf16[1,1024,768]{2,1,0:T(8,128)(2,1)S(1)}, bf16[1,1024,768]{2,1,0:T(8,128)(2,1)}, u32[]{:S(2)}) copy-start(bf16[1,1024,768]{2,1,0:T(8,128)(2,1)} %param.34) | copy-start | bytes 4718596
  8.9 44.1 %copy-start.17 = (bf16[56,3072]{1,0:T(8,128)(2,1)}, bf16[56,3072]{1,0:T(8,128)(2,1)S(1)}, u32[]{:S(2)}) copy-start(bf16[56,3072]{1,0:T(8,128)(2,1)S(1)} %fusion.84.refs_0_) | copy-start | bytes 1032196
  8.9 11.3 %collective-permute-start.1 = (bf16[56,3072]{1,0:T(8,128)(2,1)S(1)}, bf16[56,3072]{1,0:T(8,128)(2,1)}, u32[]{:S(2)}, u32[]{:S(2)}) collective-permute-start(bf16[56,3072]{1,0:T(8,128)(2,1)S(1)} %fusion.84.refs_0_), channel_id=1, source_target_pairs={{8,0},{16,8},{24,16},{28,24},{20,28},{12,20},{4,12},{0,4},{9,1},{1... | collective-permute-start | bytes 1032200 | tf_op jit(solution)/shard_map/ppermute | solution.py:190
  11.9 9.9 %collective-permute-start = (bf16[56,3072]{1,0:T(8,128)(2,1)S(1)}, bf16[56,3072]{1,0:T(8,128)(2,1)}, u32[]{:S(2)}, u32[]{:S(2)}) collective-permute-start(bf16[56,3072]{1,0:T(8,128)(2,1)S(1)} %fusion.84.refs_0_), channel_id=1, source_target_pairs={{0,8},{8,16},{16,24},{24,28},{28,20},{20,12},{12,4},{4,0},{1,9},{9... | collective-permute-start | bytes 1032200 | tf_op jit(solution)/shard_map/ppermute | solution.py:189
  20.1 9.4 %collective-permute-start.3 = (bf16[56,3072]{1,0:T(8,128)(2,1)}, bf16[56,3072]{1,0:T(8,128)(2,1)S(1)}, u32[]{:S(2)}, u32[]{:S(2)}) collective-permute-start(bf16[56,3072]{1,0:T(8,128)(2,1)} %collective-permute-done.1.refs_2_), channel_id=1, source_target_pairs={{8,0},{16,8},{24,16},{28,24},{20,28},{12,20},{4,12},{0,4},{9,1},{1... | collective-permute-start | bytes 1032200 | tf_op jit(solution)/shard_map/ppermute | solution.py:190
  21.8 9.2 %collective-permute-start.2 = (bf16[56,3072]{1,0:T(8,128)(2,1)}, bf16[56,3072]{1,0:T(8,128)(2,1)}, u32[]{:S(2)}, u32[]{:S(2)}) collective-permute-start(bf16[56,3072]{1,0:T(8,128)(2,1)} %collective-permute-done.refs_1_), channel_id=1, source_target_pairs={{0,8},{8,16},{16,24},{24,28},{28,20},{20,12},{12,4},{4,0},{1,9},{9... | collective-permute-start | bytes 1032200 | tf_op jit(solution)/shard_map/ppermute | solution.py:189
  29.6 16.0 %copy-start.23 = (bf16[56,3072]{1,0:T(8,128)(2,1)}, bf16[56,3072]{1,0:T(8,128)(2,1)S(1)}, u32[]{:S(2)}) copy-start(bf16[56,3072]{1,0:T(8,128)(2,1)S(1)} %collective-permute-done.3.refs_4_) | copy-start | bytes 1032196
  29.6 16.0 %collective-permute-start.5 = (bf16[56,3072]{1,0:T(8,128)(2,1)S(1)}, bf16[56,3072]{1,0:T(8,128)(2,1)S(1)}, u32[]{:S(2)}, u32[]{:S(2)}) collective-permute-start(bf16[56,3072]{1,0:T(8,128)(2,1)S(1)} %collective-permute-done.3.refs_4_), channel_id=1, source_target_pairs={{8,0},{16,8},{24,16},{28,24},{20,28},{12,20},{4,12},{0,4},{9,1},{1... | collective-permute-start | bytes 1032200 | tf_op jit(solution)/shard_map/ppermute | solution.py:190
  31.0 14.6 %collective-permute-start.4 = (bf16[56,3072]{1,0:T(8,128)(2,1)}, bf16[56,3072]{1,0:T(8,128)(2,1)S(1)}, u32[]{:S(2)}, u32[]{:S(2)}) collective-permute-start(bf16[56,3072]{1,0:T(8,128)(2,1)} %collective-permute-done.2.refs_3_), channel_id=1, source_target_pairs={{0,8},{8,16},{16,24},{24,28},{28,20},{20,12},{12,4},{4,0},{1,9},{9... | collective-permute-start | bytes 1032200 | tf_op jit(solution)/shard_map/ppermute | solution.py:189
  31.6 21.5 %collective-permute-start.7 = (bf16[56,3072]{1,0:T(8,128)(2,1)S(1)}, bf16[56,3072]{1,0:T(8,128)(2,1)}, u32[]{:S(2)}, u32[]{:S(2)}) collective-permute-start(bf16[56,3072]{1,0:T(8,128)(2,1)S(1)} %fusion.84.refs_0_), channel_id=1, source_target_pairs={{0,1},{1,0},{2,3},{3,2},{4,5},{5,4},{6,7},{7,6},{8,9},{9,8},{10,11... | collective-permute-start | bytes 1032200 | tf_op jit(solution)/shard_map/ppermute | solution.py:176
  44.9 8.6 %collective-permute-start.9 = (bf16[56,3072]{1,0:T(8,128)(2,1)}, bf16[56,3072]{1,0:T(8,128)(2,1)}, u32[]{:S(2)}, u32[]{:S(2)}) collective-permute-start(bf16[56,3072]{1,0:T(8,128)(2,1)} %collective-permute-done.1.refs_2_), channel_id=1, source_target_pairs={{0,1},{1,0},{2,3},{3,2},{4,5},{5,4},{6,7},{7,6},{8,9},{9,8},{10,11... | collective-permute-start | bytes 1032200 | tf_op jit(solution)/shard_map/ppermute | solution.py:176
  45.5 8.1 collective-permute-start.8
  45.6 8.4 %collective-permute-start.6 = (bf16[56,3072]{1,0:T(8,128)(2,1)S(1)}, bf16[56,3072]{1,0:T(8,128)(2,1)}, u32[]{:S(2)}, u32[]{:S(2)}) collective-permute-start(bf16[56,3072]{1,0:T(8,128)(2,1)S(1)} %broadcast_select_fusion.1), channel_id=1, source_target_pairs={{0,8},{8,16},{16,24},{24,28},{28,20},{20,12},{12,4},{4,0},{9,1},{1... | collective-permute-start | bytes 1032200 | tf_op jit(solution)/shard_map/ppermute | solution.py:201
  52.9 2.3 collective-permute-start.11
  53.1 2.3 collective-permute-start.10
  53.5 2.3 collective-permute-start.13
  53.6 2.7 collective-permute-start.12
  54.0 3.3 collective-permute-start.14
  55.2 162.7 %copy-start.12 = (bf16[96,3072]{1,0:T(8,128)(2,1)}, bf16[96,3072]{1,0:T(8,128)(2,1)S(1)}, u32[]{:S(2)}) copy-start(bf16[96,3072]{1,0:T(8,128)(2,1)S(1)} %maximum_maximum_fusion.refs_0_) | copy-start | bytes 1769476
  215.2 15.5 %collective-permute-start.16 = (bf16[96,3072]{1,0:T(8,128)(2,1)S(1)}, bf16[96,3072]{1,0:T(8,128)(2,1)S(1)}, u32[]{:S(2)}, u32[]{:S(2)}) collective-permute-start(bf16[96,3072]{1,0:T(8,128)(2,1)S(1)} %maximum_maximum_fusion.refs_0_), channel_id=1, source_target_pairs={{8,0},{16,8},{24,16},{28,24},{20,28},{12,20},{4,12},{0,4},{9,1},{1... | collective-permute-start | bytes 1769480 | tf_op jit(solution)/shard_map/ppermute | solution.py:190
  216.5 15.6 %collective-permute-start.15 = (bf16[96,3072]{1,0:T(8,128)(2,1)S(1)}, bf16[96,3072]{1,0:T(8,128)(2,1)S(1)}, u32[]{:S(2)}, u32[]{:S(2)}) collective-permute-start(bf16[96,3072]{1,0:T(8,128)(2,1)S(1)} %maximum_maximum_fusion.refs_0_), channel_id=1, source_target_pairs={{0,8},{8,16},{16,24},{24,28},{28,20},{20,12},{12,4},{4,0},{1,9},{9... | collective-permute-start | bytes 1769480 | tf_op jit(solution)/shard_map/ppermute | solution.py:189
  217.9 63.4 %collective-permute-start.22 = (bf16[96,3072]{1,0:T(8,128)(2,1)S(1)}, bf16[96,3072]{1,0:T(8,128)(2,1)}, u32[]{:S(2)}, u32[]{:S(2)}) collective-permute-start(bf16[96,3072]{1,0:T(8,128)(2,1)S(1)} %maximum_maximum_fusion.refs_0_), channel_id=1, source_target_pairs={{0,1},{1,0},{2,3},{3,2},{4,5},{5,4},{6,7},{7,6},{8,9},{9,8},{10,11... | collective-permute-start | bytes 1769480 | tf_op jit(solution)/shard_map/ppermute | solution.py:176
  230.6 14.6 %collective-permute-start.18 = (bf16[96,3072]{1,0:T(8,128)(2,1)S(1)}, bf16[96,3072]{1,0:T(8,128)(2,1)}, u32[]{:S(2)}, u32[]{:S(2)}) collective-permute-start(bf16[96,3072]{1,0:T(8,128)(2,1)S(1)} %collective-permute-done.16.refs_2_), channel_id=1, source_target_pairs={{8,0},{16,8},{24,16},{28,24},{20,28},{12,20},{4,12},{0,4},{9,1},{1... | collective-permute-start | bytes 1769480 | tf_op jit(solution)/shard_map/ppermute | solution.py:190
  232.1 14.8 %copy-start.19 = (bf16[96,3072]{1,0:T(8,128)(2,1)}, bf16[96,3072]{1,0:T(8,128)(2,1)S(1)}, u32[]{:S(2)}) copy-start(bf16[96,3072]{1,0:T(8,128)(2,1)S(1)} %collective-permute-done.15.refs_1_) | copy-start | bytes 1769476
  232.1 14.8 %collective-permute-start.17 = (bf16[96,3072]{1,0:T(8,128)(2,1)S(1)}, bf16[96,3072]{1,0:T(8,128)(2,1)}, u32[]{:S(2)}, u32[]{:S(2)}) collective-permute-start(bf16[96,3072]{1,0:T(8,128)(2,1)S(1)} %collective-permute-done.15.refs_1_), channel_id=1, source_target_pairs={{0,8},{8,16},{16,24},{24,28},{28,20},{20,12},{12,4},{4,0},{1,9},{9... | collective-permute-start | bytes 1769480 | tf_op jit(solution)/shard_map/ppermute | solution.py:189
  245.3 28.3 %collective-permute-start.20 = (bf16[96,3072]{1,0:T(8,128)(2,1)}, bf16[96,3072]{1,0:T(8,128)(2,1)S(1)}, u32[]{:S(2)}, u32[]{:S(2)}) collective-permute-start(bf16[96,3072]{1,0:T(8,128)(2,1)} %collective-permute-done.18.refs_4_), channel_id=1, source_target_pairs={{8,0},{16,8},{24,16},{28,24},{20,28},{12,20},{4,12},{0,4},{9,1},{1... | collective-permute-start | bytes 1769480 | tf_op jit(solution)/shard_map/ppermute | solution.py:190
  246.9 26.6 %collective-permute-start.19 = (bf16[96,3072]{1,0:T(8,128)(2,1)}, bf16[96,3072]{1,0:T(8,128)(2,1)S(1)}, u32[]{:S(2)}, u32[]{:S(2)}) collective-permute-start(bf16[96,3072]{1,0:T(8,128)(2,1)} %collective-permute-done.17.refs_3_), channel_id=1, source_target_pairs={{0,8},{8,16},{16,24},{24,28},{28,20},{20,12},{12,4},{4,0},{1,9},{9... | collective-permute-start | bytes 1769480 | tf_op jit(solution)/shard_map/ppermute | solution.py:189
  273.0 8.8 %collective-permute-start.24 = (bf16[96,3072]{1,0:T(8,128)(2,1)}, bf16[96,3072]{1,0:T(8,128)(2,1)S(1)}, u32[]{:S(2)}, u32[]{:S(2)}) collective-permute-start(bf16[96,3072]{1,0:T(8,128)(2,1)} %copy-done.18), channel_id=1, source_target_pairs={{0,1},{1,0},{2,3},{3,2},{4,5},{5,4},{6,7},{7,6},{8,9},{9,8},{10,11... | collective-permute-start | bytes 1769480 | tf_op jit(solution)/shard_map/ppermute | solution.py:176
  273.0 8.9 %collective-permute-start.23 = (bf16[96,3072]{1,0:T(8,128)(2,1)}, bf16[96,3072]{1,0:T(8,128)(2,1)S(1)}, u32[]{:S(2)}, u32[]{:S(2)}) collective-permute-start(bf16[96,3072]{1,0:T(8,128)(2,1)} %copy-done.19), channel_id=1, source_target_pairs={{0,1},{1,0},{2,3},{3,2},{4,5},{5,4},{6,7},{7,6},{8,9},{9,8},{10,11... | collective-permute-start | bytes 1769480 | tf_op jit(solution)/shard_map/ppermute | solution.py:176
  273.6 10.5 %collective-permute-start.21 = (bf16[96,3072]{1,0:T(8,128)(2,1)S(1)}, bf16[96,3072]{1,0:T(8,128)(2,1)}, u32[]{:S(2)}, u32[]{:S(2)}) collective-permute-start(bf16[96,3072]{1,0:T(8,128)(2,1)S(1)} %broadcast_select_fusion), channel_id=1, source_target_pairs={{0,8},{8,16},{16,24},{24,28},{28,20},{20,12},{12,4},{4,0},{9,1},{1... | collective-permute-start | bytes 1769480 | tf_op jit(solution)/shard_map/ppermute | solution.py:201
  281.2 7.4 collective-permute-start.26
  281.3 7.3 collective-permute-start.25
  281.8 6.8 collective-permute-start.28
  282.0 6.7 collective-permute-start.27
  284.1 4.5 collective-permute-start.29
  577.8 27.0 %slice-start.2 = ((s8[4718592]{0:T(1024)(128)(4,1)}), s8[524288]{0:T(1024)(128)(4,1)S(1)}, s32[]{:S(2)}) async-start(s8[4718592]{0:T(1024)(128)(4,1)} %bitcast.197), calls=%async_computation.2 | async-start | bytes 1048576
  681.6 21.8 %collective-permute-start.44 = (bf16[8,384,384]{2,1,0:T(8,128)(2,1)}, bf16[8,384,384]{2,1,0:T(8,128)(2,1)}, u32[]{:S(2)}, u32[]{:S(2)}) collective-permute-start(bf16[8,384,384]{2,1,0:T(8,128)(2,1)} %constant_dynamic-slice_fusion.6), channel_id=1, source_target_pairs={{0,1},{1,0},{2,3},{3,2},{4,5},{5,4},{6,7},{7,6},{8,9},{9,8},{10,11... | collective-permute-start | bytes 7077896 | tf_op jit(solution)/shard_map/ppermute | solution.py:176
  691.4 17.6 %collective-permute-start.30 = (bf16[8,104,1536]{2,1,0:T(8,128)(2,1)S(1)}, bf16[8,104,1536]{2,1,0:T(8,128)(2,1)S(1)}, u32[]{:S(2)}, u32[]{:S(2)}) collective-permute-start(bf16[8,104,1536]{2,1,0:T(8,128)(2,1)S(1)} %fusion.22), channel_id=1, source_target_pairs={{0,1},{1,0},{2,3},{3,2},{4,5},{5,4},{6,7},{7,6},{8,9},{9,8},{10,11... | collective-permute-start | bytes 7667720 | tf_op jit(solution)/shard_map/ppermute | solution.py:176
  691.5 16.1 %slice-start.4 = ((s8[4718592]{0:T(1024)(128)(4,1)}), s8[4194304]{0:T(1024)(128)(4,1)S(1)}, s32[]{:S(2)}) async-start(s8[4718592]{0:T(1024)(128)(4,1)} %bitcast.200), calls=%async_computation.4 | async-start | bytes 8388608
  693.4 14.1 %collective-permute-start.37 = (bf16[8,96,1536]{2,1,0:T(8,128)(2,1)S(1)}, bf16[8,96,1536]{2,1,0:T(8,128)(2,1)S(1)}, u32[]{:S(2)}, u32[]{:S(2)}) collective-permute-start(bf16[8,96,1536]{2,1,0:T(8,128)(2,1)S(1)} %constant_dynamic-slice_fusion.5), channel_id=1, source_target_pairs={{0,1},{1,0},{2,3},{3,2},{4,5},{5,4},{6,7},{7,6},{8,9},{9,8},{10,11... | collective-permute-start | bytes 7077896 | tf_op jit(solution)/shard_map/ppermute | solution.py:176
  694.3 13.3 %slice-start.5 = ((s8[4718592]{0:T(1024)(128)(4,1)}), s8[524288]{0:T(1024)(128)(4,1)S(1)}, s32[]{:S(2)}) async-start(s8[4718592]{0:T(1024)(128)(4,1)} %bitcast.200), calls=%async_computation.5 | async-start | bytes 1048576
  705.8 28.9 %collective-permute-start.45 = (bf16[4,384,384]{2,1,0:T(8,128)(2,1)S(1)}, bf16[4,384,384]{2,1,0:T(8,128)(2,1)S(1)}, u32[]{:S(2)}, u32[]{:S(2)}) collective-permute-start(bf16[4,384,384]{2,1,0:T(8,128)(2,1)S(1)} %fusion.64), channel_id=1, source_target_pairs={{0,4},{4,0},{8,12},{12,8},{16,20},{20,16},{24,28},{28,24},{1,5},{5... | collective-permute-start | bytes 3538952 | tf_op jit(solution)/shard_map/ppermute | solution.py:276
  708.5 51.5 %collective-permute-start.38 = (bf16[4,96,1536]{2,1,0:T(8,128)(2,1)S(1)}, bf16[4,96,1536]{2,1,0:T(8,128)(2,1)S(1)}, u32[]{:S(2)}, u32[]{:S(2)}) collective-permute-start(bf16[4,96,1536]{2,1,0:T(8,128)(2,1)S(1)} %fusion.63), channel_id=1, source_target_pairs={{0,4},{4,0},{8,12},{12,8},{16,20},{20,16},{24,28},{28,24},{1,5},{5... | collective-permute-start | bytes 3538952 | tf_op jit(solution)/shard_map/ppermute | solution.py:276
  710.0 80.3 %collective-permute-start.31 = (bf16[4,104,1536]{2,1,0:T(8,128)(2,1)S(1)}, bf16[4,104,1536]{2,1,0:T(8,128)(2,1)S(1)}, u32[]{:S(2)}, u32[]{:S(2)}) collective-permute-start(bf16[4,104,1536]{2,1,0:T(8,128)(2,1)S(1)} %fusion.62), channel_id=1, source_target_pairs={{0,4},{4,0},{8,12},{12,8},{16,20},{20,16},{24,28},{28,24},{1,5},{5... | collective-permute-start | bytes 3833864 | tf_op jit(solution)/shard_map/ppermute | solution.py:276
  735.0 27.0 %collective-permute-start.46 = (bf16[384,384]{1,0:T(8,128)(2,1)S(1)}, bf16[384,384]{1,0:T(8,128)(2,1)S(1)}, u32[]{:S(2)}, u32[]{:S(2)}) collective-permute-start(bf16[384,384]{1,0:T(8,128)(2,1)S(1)} %get-tuple-element.54), channel_id=1, source_target_pairs={{0,8},{4,12},{8,0},{12,4},{16,24},{20,28},{24,16},{28,20},{1,9},{5... | collective-permute-start | bytes 884744 | tf_op jit(solution)/shard_map/ppermute | solution.py:282
  736.7 27.9 %collective-permute-start.48 = (bf16[384,384]{1,0:T(8,128)(2,1)S(1)}, bf16[384,384]{1,0:T(8,128)(2,1)S(1)}, u32[]{:S(2)}, u32[]{:S(2)}) collective-permute-start(bf16[384,384]{1,0:T(8,128)(2,1)S(1)} %get-tuple-element.55), channel_id=1, source_target_pairs={{0,24},{4,28},{8,16},{12,20},{16,8},{20,12},{24,0},{28,4},{1,25},{... | collective-permute-start | bytes 884744 | tf_op jit(solution)/shard_map/ppermute | solution.py:282
  739.2 25.5 %copy-start.7 = (f32[1024,768]{1,0:T(8,128)S(1)}, f32[1024,768]{1,0:T(8,128)}, u32[]{:S(2)}) copy-start(f32[1024,768]{1,0:T(8,128)} %copy-done.6) | copy-start | bytes 9437188
  739.2 25.5 %copy-start.11 = (f32[1024,768]{1,0:T(8,128)S(1)}, f32[1024,768]{1,0:T(8,128)}, u32[]{:S(2)}) copy-start(f32[1024,768]{1,0:T(8,128)} %get-tuple-element.97) | copy-start | bytes 9437188
  739.2 27.9 %collective-permute-start.47 = (bf16[384,384]{1,0:T(8,128)(2,1)S(1)}, bf16[384,384]{1,0:T(8,128)(2,1)S(1)}, u32[]{:S(2)}, u32[]{:S(2)}) collective-permute-start(bf16[384,384]{1,0:T(8,128)(2,1)S(1)} %get-tuple-element.56), channel_id=1, source_target_pairs={{0,16},{4,20},{8,24},{12,28},{16,0},{20,4},{24,8},{28,12},{1,17},{... | collective-permute-start | bytes 884744 | tf_op jit(solution)/shard_map/ppermute | solution.py:282
  760.4 15.3 %collective-permute-start.39 = (bf16[96,1536]{1,0:T(8,128)(2,1)S(1)}, bf16[96,1536]{1,0:T(8,128)(2,1)S(1)}, u32[]{:S(2)}, u32[]{:S(2)}) collective-permute-start(bf16[96,1536]{1,0:T(8,128)(2,1)S(1)} %get-tuple-element.57), channel_id=1, source_target_pairs={{0,8},{4,12},{8,0},{12,4},{16,24},{20,28},{24,16},{28,20},{1,9},{5... | collective-permute-start | bytes 884744 | tf_op jit(solution)/shard_map/ppermute | solution.py:282
  762.1 16.7 %collective-permute-start.41 = (bf16[96,1536]{1,0:T(8,128)(2,1)S(1)}, bf16[96,1536]{1,0:T(8,128)(2,1)S(1)}, u32[]{:S(2)}, u32[]{:S(2)}) collective-permute-start(bf16[96,1536]{1,0:T(8,128)(2,1)S(1)} %get-tuple-element.58), channel_id=1, source_target_pairs={{0,24},{4,28},{8,16},{12,20},{16,8},{20,12},{24,0},{28,4},{1,25},{... | collective-permute-start | bytes 884744 | tf_op jit(solution)/shard_map/ppermute | solution.py:282
  764.6 24.1 %collective-permute-start.40 = (bf16[96,1536]{1,0:T(8,128)(2,1)S(1)}, bf16[96,1536]{1,0:T(8,128)(2,1)S(1)}, u32[]{:S(2)}, u32[]{:S(2)}) collective-permute-start(bf16[96,1536]{1,0:T(8,128)(2,1)S(1)} %get-tuple-element.59), channel_id=1, source_target_pairs={{0,16},{4,20},{8,24},{12,28},{16,0},{20,4},{24,8},{28,12},{1,17},{... | collective-permute-start | bytes 884744 | tf_op jit(solution)/shard_map/ppermute | solution.py:282
  767.2 27.1 %collective-permute-start.49 = (bf16[384,384]{1,0:T(8,128)(2,1)S(1)}, bf16[384,384]{1,0:T(8,128)(2,1)S(1)}, u32[]{:S(2)}, u32[]{:S(2)}) collective-permute-start(bf16[384,384]{1,0:T(8,128)(2,1)S(1)} %fusion.79), channel_id=1, source_target_pairs={{0,2},{1,3},{2,0},{3,1},{4,6},{5,7},{6,4},{7,5},{8,10},{9,11},{10,... | collective-permute-start | bytes 884744 | tf_op jit(solution)/shard_map/ppermute | solution.py:285
  788.8 6.8 collective-permute-start.42
  790.8 13.1 %collective-permute-start.32 = (bf16[104,1536]{1,0:T(8,128)(2,1)S(1)}, bf16[104,1536]{1,0:T(8,128)(2,1)S(1)}, u32[]{:S(2)}, u32[]{:S(2)}) collective-permute-start(bf16[104,1536]{1,0:T(8,128)(2,1)S(1)} %get-tuple-element.51), channel_id=1, source_target_pairs={{0,8},{4,12},{8,0},{12,4},{16,24},{20,28},{24,16},{28,20},{1,9},{5... | collective-permute-start | bytes 958472 | tf_op jit(solution)/shard_map/ppermute | solution.py:282
  790.9 17.8 %collective-permute-start.34 = (bf16[104,1536]{1,0:T(8,128)(2,1)S(1)}, bf16[104,1536]{1,0:T(8,128)(2,1)S(1)}, u32[]{:S(2)}, u32[]{:S(2)}) collective-permute-start(bf16[104,1536]{1,0:T(8,128)(2,1)S(1)} %get-tuple-element.52), channel_id=1, source_target_pairs={{0,24},{4,28},{8,16},{12,20},{16,8},{20,12},{24,0},{28,4},{1,25},{... | collective-permute-start | bytes 958472 | tf_op jit(solution)/shard_map/ppermute | solution.py:282
  793.6 25.6 %collective-permute-start.33 = (bf16[104,1536]{1,0:T(8,128)(2,1)S(1)}, bf16[104,1536]{1,0:T(8,128)(2,1)S(1)}, u32[]{:S(2)}, u32[]{:S(2)}) collective-permute-start(bf16[104,1536]{1,0:T(8,128)(2,1)S(1)} %get-tuple-element.53), channel_id=1, source_target_pairs={{0,16},{4,20},{8,24},{12,28},{16,0},{20,4},{24,8},{28,12},{1,17},{... | collective-permute-start | bytes 958472 | tf_op jit(solution)/shard_map/ppermute | solution.py:282
  794.4 25.6 %collective-permute-start.50 = (bf16[384,384]{1,0:T(8,128)(2,1)S(1)}, bf16[384,384]{1,0:T(8,128)(2,1)S(1)}, u32[]{:S(2)}, u32[]{:S(2)}) collective-permute-start(bf16[384,384]{1,0:T(8,128)(2,1)S(1)} %add_convert_fusion.4), channel_id=1, source_target_pairs={{0,1},{1,0},{2,3},{3,2},{4,5},{5,4},{6,7},{7,6},{8,9},{9,8},{10,11... | collective-permute-start | bytes 884744 | tf_op jit(solution)/shard_map/ppermute | solution.py:176
  795.6 25.5 %collective-permute-start.43 = (bf16[96,1536]{1,0:T(8,128)(2,1)S(1)}, bf16[96,1536]{1,0:T(8,128)(2,1)S(1)}, u32[]{:S(2)}, u32[]{:S(2)}) collective-permute-start(bf16[96,1536]{1,0:T(8,128)(2,1)S(1)} %add_convert_fusion.5), channel_id=1, source_target_pairs={{0,1},{1,0},{2,3},{3,2},{4,5},{5,4},{6,7},{7,6},{8,9},{9,8},{10,11... | collective-permute-start | bytes 884744 | tf_op jit(solution)/shard_map/ppermute | solution.py:176
  819.4 7.1 collective-permute-start.35
  826.5 1.7 collective-permute-start.36
  (39 other events, 195.2 us)
